TPU v7x, 256 devices: a whole 4x4x8 slice. The times are simulated.
256 devices in a mesh: pipe: 8 (over x, core), vocab: 32 (over z, y).
Axes of the slice: x: 4, y: 4, z: 8, core: 2. Of those that a mesh axis runs over, the one named last changes fastest.
Arguments:
- hidden: bfloat16 [8, 128, 4096], P('pipe'), may hold values from -60 to 60
- norm_gain: float32 [4096], replicated, may hold values from 0.5 to 1.5
- out_weight: bfloat16 [128256, 4096], P(('pipe', 'vocab')), may hold values from -4 to 4
- targets: int32 [8, 128], P('pipe'), may hold values from 0 to 128255
- loss_mask: int32 [8, 128], P('pipe'), may hold values from 0 to 1, as said below
- slot_position: int32 [8, 128], P('pipe'), may hold values from 0 to 127, each once within a row
- counts: int32 [8], replicated, may hold values from 1 to 128, 640 in all
- loss_scale: float32 [], replicated, may hold values from 4096 to 32768
Outputs:
- loss: float32 [], replicated
- grad_hidden: bfloat16 [8, 128, 4096], P('pipe')
Inputs may be any that keep to these rules, and one draw needn't show every extreme that they name: The 8 counts sum to exactly 640, and one of them equals 128. Each row of slot_position holds every number of 0 to 127 once. Each row of loss_mask holds at least 64 ones.
All inputs are finite; a program needn't handle non-finite values.
Results may differ from a plain program's by a relative error of at most 0.0034.
Values may be sent and summed in bfloat16 or wider, within the bound.
No kernel may reach another device: no remote copies, remote signals or barrier semaphores. Data moves between devices by JAX's collectives and lax.ppermute only.
A program may use at most 64 MiB of HBM per device.

v0:
```python
import jax
import jax.numpy as jnp
from jax import lax
from jax.experimental import pallas as pl
from jax.experimental.pallas import tpu as pltpu
from jax.sharding import Mesh
from jax.sharding import PartitionSpec as P

AXES = ("x", "c", "z", "y")
SIZE = {"x": 4, "c": 2, "z": 8, "y": 4}
PIPE = ("x", "c")
LIVE = 640
EPSILON = 1e-05
BF16, F16, F32 = jnp.bfloat16, jnp.float16, jnp.float32


def shift(value, axis, by):
    n = SIZE[axis]
    return lax.ppermute(value, axis, [(i, (i + by) % n) for i in range(n)])


def swap_cores(value):
    return lax.ppermute(value, "c", [(0, 1), (1, 0)])


def place(pieces, axis):
    own = lax.axis_index(axis)
    out = jnp.zeros((4,) + pieces[0].shape, pieces[0].dtype)
    for k, piece in enumerate(pieces):
        out = lax.dynamic_update_index_in_dim(out, piece, (own + k) % 4, 0)
    return out


def gather_ring(chunk, axis):
    half = chunk.shape[0] // 2
    below, above = shift(chunk, axis, 1), shift(chunk, axis, -1)
    first, second = shift(below[:half], axis, 1), shift(above[half:], axis, -1)
    return [chunk, above, jnp.concatenate([first, second], 0), below]


def pick(chunks, axis, k):
    own = lax.axis_index(axis)
    return lax.dynamic_index_in_dim(chunks, (own + k) % 4, 0, keepdims=False)


def scatter_direct(chunks, axis):
    got = [shift(pick(chunks, axis, k).astype(F16), axis, k) for k in (1, 2, 3)]
    total = pick(chunks, axis, 0)
    for g in got:
        total = total + g.astype(F32)
    return total


def scatter_ring(chunks, axis):
    half = chunks.shape[1] // 2
    far = pick(chunks, axis, 2).astype(F16)
    first, second = shift(far[:half], axis, 1), shift(far[half:], axis, -1)
    up, down = pick(chunks, axis, 1), pick(chunks, axis, 3)
    up = jnp.concatenate([up[:half] + first.astype(F32), up[half:]], 0).astype(F16)
    down = jnp.concatenate([down[:half], down[half:] + second.astype(F32)], 0).astype(F16)
    got_below, got_above = shift(up, axis, 1), shift(down, axis, -1)
    return pick(chunks, axis, 0) + got_below.astype(F32) + got_above.astype(F32)


def exchange(value, axes):
    return lax.all_to_all(value, axes, 0, 0)


def everyone(value, axes):
    n = 1
    for a in axes:
        n *= SIZE[a]
    return exchange(jnp.broadcast_to(value[None], (n,) + value.shape), axes)


def merge(stats):
    top = jnp.max(stats[:, 0], axis=0)
    total = jnp.sum(stats[:, 1] * jnp.exp(stats[:, 0] - top[None]), axis=0)
    return jnp.stack([top, total, jnp.sum(stats[:, 2], axis=0)])


NT = (((1,), (1,)), ((), ()))
TN = (((0,), (0,)), ((), ()))
MIB = 1024 * 1024
VM, SM = pl.BlockSpec(memory_space=pltpu.VMEM), pl.BlockSpec(memory_space=pltpu.SMEM)


def slice_kernel(y_ref, h_ref, gain_ref, target_ref, mask_ref, position_ref, out_ref, scales):
    slots, width = h_ref.shape
    half, quarter = width // 2, width // 4

    def step(i, carry):
        at = pl.ds(pl.multiple_of(i * 16, 16), 16)
        values = h_ref[at, :].astype(F32)
        mean = jnp.sum(values * values, axis=1, keepdims=True) / width
        scales[at, :] = jnp.broadcast_to(lax.rsqrt(mean + EPSILON), (16, 128))
        return carry

    lax.fori_loop(0, slots // 16, step, 0)

    def tile(offset):
        at = pl.ds(pl.multiple_of(offset, 128), 128)
        return (h_ref[:, at].astype(F32) * scales[...] * gain_ref[:, at]).T.astype(BF16)

    word = target_ref[...]
    rows = [word & 255, (word >> 8) & 255, word >> 16, mask_ref[...], position_ref[...]]
    info = jnp.concatenate(rows + [jnp.zeros_like(word)] * 11, 0).astype(F32).astype(BF16)

    def fill(core, carry):
        for part in range(2):
            for x in range(4):
                out_ref[x * 2 + core, part * 128 : part * 128 + 128, :] = tile(core * half + x * 256 + part * 128)
                out_ref[x * 2 + core, 512:528, :] = info
            second = tile(core * half + quarter + y_ref[0] * 256 + part * 128)
            for x in range(4):
                out_ref[x * 2 + core, 256 + part * 128 : 384 + part * 128, :] = second
        return carry

    lax.fori_loop(0, 2, fill, 0)


def slices_of(y, rows, gain, targets, mask, position):
    slots, width = rows.shape
    return pl.pallas_call(
        slice_kernel,
        name="normed_slices",
        out_shape=jax.ShapeDtypeStruct((8, 528, slots), BF16),
        in_specs=[SM] + [VM] * 5,
        out_specs=VM,
        scratch_shapes=[pltpu.VMEM((slots, 128), F32)],
        cost_estimate=pl.CostEstimate(flops=4 * slots * width, bytes_accessed=4 * slots * width, transcendentals=slots),
    )(y, rows, gain.reshape(1, width), targets, mask, position)


def compact_kernel(offset_ref, loss_scale_ref, counts_ref, packed_ref, one_ref, two_ref, word_ref, column_ref, coef_ref, count_ref, acc):
    iota = lambda shape, axis: lax.broadcasted_iota(jnp.int32, shape, axis)
    rows = []
    for micro in range(8):
        codes = packed_ref[micro, 512:528, :].astype(F32)
        rows.append(((codes[4:5] < counts_ref[micro].astype(F32)) & (codes[3:4] == 1.0)).astype(F32))
    live = jnp.concatenate(rows, 0)
    before = jnp.dot(
        live.astype(BF16),
        jnp.where(iota((128, 128), 0) < iota((128, 128), 1), 1.0, 0.0).astype(BF16),
        preferred_element_type=F32,
    )
    per_micro = jnp.sum(live, axis=1, keepdims=True)
    base = [jnp.zeros((1, 1), F32)]
    for micro in range(8):
        base.append(base[-1] + per_micro[micro : micro + 1])
    count = base.pop()
    column = jnp.where(live > 0.0, before + jnp.concatenate(base, 0), -1.0).astype(jnp.int32)
    column_ref[...] = column
    spot = iota((8, 128), 0) * 128 + iota((8, 128), 1)
    coef_ref[...] = jnp.where(spot.astype(F32) < count, loss_scale_ref[0] / count, 0.0)
    count_ref[...] = jnp.broadcast_to(count, (8, 128))
    for n in range(4):
        values = jnp.concatenate([packed_ref[2 * n], packed_ref[2 * n + 1]], 1)
        places = [
            jnp.where(iota((LIVE, 128), 0) == column[m : m + 1], 1.0, 0.0).astype(BF16) for m in (2 * n, 2 * n + 1)
        ]
        part = lax.dot_general(values, jnp.concatenate(places, 1), NT, preferred_element_type=F32)
        acc[...] = part if n == 0 else acc[...] + part
    one_ref[...] = acc[0:256, :].astype(BF16)
    two_ref[...] = acc[256:512, :].astype(BF16)
    word = acc[512:513, :] + 256.0 * acc[513:514, :] + 65536.0 * acc[514:515, :]
    word_ref[...] = word.astype(jnp.int32) - offset_ref[0]


def compact_of(offset, loss_scale, counts, packed):
    tile, whole = jax.ShapeDtypeStruct((8, 128), F32), jax.ShapeDtypeStruct((8, 128), jnp.int32)
    wide = jax.ShapeDtypeStruct((256, LIVE), BF16)
    return pl.pallas_call(
        compact_kernel,
        name="compact",
        out_shape=(wide, wide, jax.ShapeDtypeStruct((1, LIVE), jnp.int32), whole, tile, tile),
        in_specs=[SM, SM, SM, VM],
        out_specs=(VM,) * 6,
        scratch_shapes=[pltpu.VMEM((528, LIVE), F32)],
        compiler_params=pltpu.CompilerParams(vmem_limit_bytes=12 * MIB),
        cost_estimate=pl.CostEstimate(flops=2 * 528 * 1024 * LIVE, bytes_accessed=3 * MIB, transcendentals=0),
    )(offset, loss_scale, counts, packed)


def product_kernel(weight_ref, one_ref, two_ref, out_ref):
    width = one_ref.shape[0]
    for at in (slice(0, 256), slice(256, 512), slice(512, 640)):
        out_ref[:, at] = jnp.dot(weight_ref[:, :width], one_ref[:, at], preferred_element_type=F32) + jnp.dot(
            weight_ref[:, width:], two_ref[:, at], preferred_element_type=F32
        )


def product(weight, one, two):
    words, width = weight.shape
    return pl.pallas_call(
        product_kernel,
        name="product",
        out_shape=jax.ShapeDtypeStruct((words, LIVE), F32),
        in_specs=[VM] * 3,
        out_specs=VM,
        compiler_params=pltpu.CompilerParams(vmem_limit_bytes=10 * MIB),
        cost_estimate=pl.CostEstimate(flops=2 * words * width * LIVE, bytes_accessed=6 * MIB, transcendentals=0),
    )(weight, one, two)


def pull_kernel(mine_ref, other_ref, grad_ref, other_grad_ref, out_ref):
    def step(i, carry):
        at = pl.ds(pl.multiple_of(i * 256, 256), 256)
        out_ref[at, :] = lax.dot_general(
            mine_ref[:, at], grad_ref[...], TN, preferred_element_type=F32
        ) + lax.dot_general(other_ref[:, at], other_grad_ref[...], TN, preferred_element_type=F32)
        return carry

    lax.fori_loop(0, out_ref.shape[0] // 256, step, 0)


def pull(mine, other, grad, other_grad):
    words, width = mine.shape
    return pl.pallas_call(
        pull_kernel,
        name="pull",
        out_shape=jax.ShapeDtypeStruct((width, LIVE), F32),
        in_specs=[VM] * 4,
        out_specs=VM,
        compiler_params=pltpu.CompilerParams(vmem_limit_bytes=14 * MIB),
        cost_estimate=pl.CostEstimate(flops=4 * words * width * LIVE, bytes_accessed=12 * MIB, transcendentals=0),
    )(mine, other, grad, other_grad)


def stats_kernel(count_ref, own_ref, other_ref, word_ref, logit_ref, stat_ref):
    words = own_ref.shape[0]
    total = jnp.zeros((1, 128), F32)
    for t in range(LIVE // 128):
        at = slice(t * 128, t * 128 + 128)
        logits = own_ref[:, at] + other_ref[:, at]
        logit_ref[:, at] = logits
        top = jnp.max(logits, axis=0, keepdims=True)
        stat_ref[t : t + 1, :] = top + jnp.log(jnp.sum(jnp.exp(logits - top), axis=0, keepdims=True))
        hit = lax.broadcasted_iota(jnp.int32, (words, 128), 0) == word_ref[:, at]
        chosen = jnp.sum(jnp.where(hit, logits, 0.0), axis=0, keepdims=True)
        spot = lax.broadcasted_iota(jnp.int32, (1, 128), 1) + t * 128
        total = total + jnp.where(spot.astype(F32) < count_ref[0], chosen, 0.0)
    stat_ref[5:8, :] = jnp.broadcast_to(jnp.sum(total, axis=1, keepdims=True), (3, 128))


def stats_of(count, own, other, word):
    words = own.shape[0]
    return pl.pallas_call(
        stats_kernel,
        name="stats",
        compiler_params=pltpu.CompilerParams(vmem_limit_bytes=6 * MIB),
        out_shape=(jax.ShapeDtypeStruct((words, LIVE), F32), jax.ShapeDtypeStruct((8, 128), F32)),
        in_specs=[SM] + [VM] * 3,
        out_specs=(VM, VM),
        cost_estimate=pl.CostEstimate(flops=8 * words * LIVE, bytes_accessed=12 * words * LIVE, transcendentals=words * LIVE),
    )(count, own, other, word)


def grad_kernel(logit_ref, total_ref, coef_ref, word_ref, out_ref):
    words = logit_ref.shape[0]
    for t in range(LIVE // 128):
        at = slice(t * 128, t * 128 + 128)
        hit = lax.broadcasted_iota(jnp.int32, (words, 128), 0) == word_ref[:, at]
        value = (jnp.exp(logit_ref[:, at] - total_ref[t : t + 1, :]) - hit.astype(F32)) * coef_ref[t : t + 1, :]
        out_ref[:, at] = value.astype(BF16)


def grad_of(logits, total, coef, word):
    words = logits.shape[0]
    return pl.pallas_call(
        grad_kernel,
        name="logit_grad",
        compiler_params=pltpu.CompilerParams(vmem_limit_bytes=4 * MIB),
        out_shape=jax.ShapeDtypeStruct((words, LIVE), BF16),
        in_specs=[VM] * 4,
        out_specs=VM,
        cost_estimate=pl.CostEstimate(flops=4 * words * LIVE, bytes_accessed=6 * words * LIVE, transcendentals=words * LIVE),
    )(logits, total, coef, word)


def finish_kernel(grad_ref, h_ref, gain_ref, out_ref, turned):
    slots, width = h_ref.shape
    for core in range(2):
        for part in range(2):
            for a in range(4):
                for b in range(2):
                    blocks = []
                    for pair in range(2):
                        for z in range(8):
                            other = 2 * b + pair
                            y, x = (other, a) if part == 0 else (a, other)
                            blocks.append(grad_ref[y, z, x, core, part])
                    at = core * (width // 2) + part * (width // 4) + a * 256 + b * 128
                    turned[:, at : at + 128] = jnp.concatenate(blocks, 0).T

    def step(i, carry):
        at = pl.ds(pl.multiple_of(i * 16, 16), 16)
        values = h_ref[at, :].astype(F32)
        scale = lax.rsqrt(jnp.sum(values * values, axis=1, keepdims=True) / width + EPSILON)
        pulled = turned[at, :] * gain_ref[...]
        inner = jnp.sum(values * pulled, axis=1, keepdims=True) / width
        out_ref[at, :] = (scale * pulled - scale * scale * scale * values * inner).astype(BF16)
        return carry

    lax.fori_loop(0, slots // 16, step, 0)


def finish(grad, rows, gain):
    slots, width = rows.shape
    vmem = pl.BlockSpec(memory_space=pltpu.VMEM)
    return pl.pallas_call(
        finish_kernel,
        out_shape=jax.ShapeDtypeStruct((slots, width), BF16),
        in_specs=[vmem] * 3,
        out_specs=vmem,
        scratch_shapes=[pltpu.VMEM((slots, width), F32)],
        compiler_params=pltpu.CompilerParams(vmem_limit_bytes=16 * MIB),
        cost_estimate=pl.CostEstimate(flops=8 * slots * width, bytes_accessed=8 * slots * width, transcendentals=slots),
    )(grad, rows, gain.reshape(1, width))


def merge_rows(rows):
    top = jnp.max(rows, axis=0)
    joined = top + jnp.log(jnp.sum(jnp.exp(rows - top[None]), axis=0))
    return jnp.where(jnp.arange(8)[:, None] < 5, joined, jnp.sum(rows, axis=0))


def body(hidden, norm_gain, out_weight, targets, loss_mask, slot_position, counts, loss_scale):
    slots, width = hidden.shape[1], hidden.shape[2]
    words = out_weight.shape[0]
    core, y = lax.axis_index("c"), lax.axis_index("y")
    offset = lax.axis_index(AXES) * words
    half = width // 2
    raw = hidden.reshape(slots, width)
    packed = slices_of(y.reshape(1).astype(jnp.int32), raw, norm_gain, targets, loss_mask, slot_position)
    packed, late_weight = lax.optimization_barrier((packed, out_weight))
    packed = exchange(packed, PIPE)
    mine = lax.dynamic_slice_in_dim(late_weight, core * half, half, 1)
    other = swap_cores(lax.dynamic_slice_in_dim(late_weight, (1 - core) * half, half, 1))

    near_one, near_two, word, column, coef, count = compact_of(
        offset.reshape(1).astype(jnp.int32), loss_scale.reshape(1), counts, packed
    )
    weight_total = count[0, 0]
    select = column.reshape(8 * slots, 1) == jnp.arange(LIVE, dtype=jnp.int32)[None, :]
    one = place(gather_ring(near_one, "x"), "x").reshape(1024, LIVE)
    two = place(gather_ring(near_two, "y"), "y").reshape(1024, LIVE)
    sib = product(other, one, two)
    sib, one, two = lax.optimization_barrier((sib, one, two))
    logits, stats = stats_of(weight_total.reshape(1), product(mine, one, two), swap_cores(sib), word)
    stats = merge_rows(everyone(stats, ("z", "y")))
    stats = merge_rows(everyone(stats, PIPE))
    weight = (jnp.arange(8 * slots, dtype=F32).reshape(8, slots) < weight_total).astype(F32)
    loss = (jnp.sum((weight * stats)[:5]) - stats[5, 0]) / weight_total
    logit_grad = grad_of(logits, stats, coef, word)
    other_grad = swap_cores(logit_grad)
    grad = pull(mine, other, logit_grad, other_grad)

    one = scatter_ring(grad[:1024].reshape(4, 256, LIVE), "x")
    two = scatter_ring(grad[1024:].reshape(4, 256, LIVE), "y")
    one = scatter_direct(one.reshape(4, 64, LIVE), "y")
    two = scatter_direct(two.reshape(4, 64, LIVE), "x")
    chunk = jnp.concatenate([one.reshape(8, 8, LIVE), two.reshape(8, 8, LIVE)], 1).reshape(128, LIVE)
    spread = lax.dot_general(
        chunk, select.astype(F32), NT, precision=lax.Precision.HIGHEST, preferred_element_type=F32
    )
    spread = spread.astype(F16).reshape(8, 16, 8, slots).transpose(2, 0, 1, 3).reshape(64, 16, slots)
    spread = exchange(spread, ("x", "c", "z")).reshape(8, 8, 16, slots)
    spread = jnp.sum(spread.astype(F32), axis=1).astype(F16).reshape(128, slots)
    full = everyone(spread, ("z",)).reshape(1024, slots)
    full = place(gather_ring(full, "y"), "y").astype(F32).reshape(4, 8, 4, 2, 2, 8, slots)
    return loss, finish(full, raw, norm_gain).reshape(1, slots, width)


def solution(mesh):
    split = Mesh(mesh.devices.reshape(4, 2, 8, 4), AXES)
    return jax.shard_map(
        body,
        mesh=split,
        in_specs=(
            P(PIPE, None, None),
            P(),
            P(AXES, None),
            P(PIPE, None),
            P(PIPE, None),
            P(PIPE, None),
            P(),
            P(),
        ),
        out_specs=(P(), P(PIPE, None, None)),
        check_vma=False,
    )
```

profile of v0, /device:TPU:24, one launch (start us, length us, event | category | flops | bytes accessed | tf_op | source)
XLA Modules:
  0.0 187.0 jit_solution(15099698791796718104)
XLA Ops:
  0.6 3.7 %normed_slices.1 = bf16[8,528,128]{2,1,0:T(8,128)(2,1)} custom-call(s32[1]{0:T(128)} %bitcast.2.y_ref, bf16[128,4096]{1,0:T(8,128)(2,1)} %bitcast.148, f32[1,4096]{1,0:T(1,128)} %bitcast.150, s32[1,128]{1,0:T(1,128)} %target_ref.1, s32[1,128]{1,0:T(1,128)} %mask_ref.1, s32[1,128]{1,0:T(1,128)} %position_ref.1), custom_call_target="tpu_custom_call" | custom-call | flops 2097152 | bytes 2097152 | tf_op jit(solution)/shard_map/normed_slices/pallas_call | solution.py:124
  4.3 4.3 %all-to-all-start = ((bf16[8,528,128]{2,1,0:T(8,128)(2,1)}), bf16[8,528,128]{2,1,0:T(8,128)(2,1)S(1)}, u32[]{:S(2)}, u32[]{:S(2)}) async-start(bf16[8,528,128]{2,1,0:T(8,128)(2,1)} %normed_slices.1), calls=%async_computation | async-start | bytes 2162688 | tf_op jit(solution)/shard_map/all_to_all | solution.py:66
  8.6 3.9 %constant_dynamic-slice_fusion = (bf16[501,2048]{1,0:T(8,128)(2,1)}, bf16[501,2048]{1,0:T(8,128)(2,1)S(1)}) fusion(bf16[501,4096]{1,0:T(8,128)(2,1)} %param.10, s32[]{:T(128)S(6)} %select_n.141, s32[]{:T(128)S(6)} %select_n.140), kind=kLoop, calls=%fused_computation.78 | loop fusion | bytes 8208392 | tf_op jit(solution)/shard_map/dynamic_slice | solution.py:339
  13.7 11.2 %all-to-all-done.packed_ref = bf16[8,528,128]{2,1,0:T(8,128)(2,1)S(1)} async-done(((bf16[8,528,128]{2,1,0:T(8,128)(2,1)}), bf16[8,528,128]{2,1,0:T(8,128)(2,1)S(1)}, u32[]{:S(2)}, u32[]{:S(2)}) %all-to-all-start) | async-done | bytes 1081376 | tf_op jit(solution)/shard_map/all_to_all | solution.py:66
  27.5 2.5 %collective-permute-start.6 = (bf16[256,640]{1,0:T(8,128)(2,1)S(1)}, bf16[256,640]{1,0:T(8,128)(2,1)S(1)}, u32[]{:S(2)}, u32[]{:S(2)}) collective-permute-start(bf16[256,640]{1,0:T(8,128)(2,1)S(1)} %get-tuple-element.19), channel_id=1, source_target_pairs={{0,1},{1,2},{2,3},{3,0},{4,5},{5,6},{6,7},{7,4},{8,9},{9,10},{10,1... | collective-permute-start | bytes 983048 | tf_op jit(solution)/shard_map/ppermute | solution.py:19
  32.3 4.1 %collective-permute-done.6 = bf16[256,640]{1,0:T(8,128)(2,1)S(1)} collective-permute-done((bf16[256,640]{1,0:T(8,128)(2,1)S(1)}, bf16[256,640]{1,0:T(8,128)(2,1)S(1)}, u32[]{:S(2)}, u32[]{:S(2)}) %collective-permute-start.6) | collective-permute-done | bytes 327712 | tf_op jit(solution)/shard_map/ppermute | solution.py:19
  36.5 3.8 %collective-permute-start.7 = (bf16[128,640]{1,0:T(8,128)(2,1)S(1)}, bf16[128,640]{1,0:T(8,128)(2,1)S(1)}, u32[]{:S(2)}, u32[]{:S(2)}) collective-permute-start(bf16[128,640]{1,0:T(8,128)(2,1)S(1)} %slice.146), channel_id=1, source_target_pairs={{0,1},{1,2},{2,3},{3,0},{4,5},{5,6},{6,7},{7,4},{8,9},{9,10},{10,1... | collective-permute-start | bytes 491528 | tf_op jit(solution)/shard_map/ppermute | solution.py:19
  41.1 3.1 %collective-permute-start.4 = (bf16[128,640]{1,0:T(8,128)(2,1)S(1)}, bf16[128,640]{1,0:T(8,128)(2,1)S(1)}, u32[]{:S(2)}, u32[]{:S(2)}) collective-permute-start(bf16[128,640]{1,0:T(8,128)(2,1)S(1)} %slice.145), channel_id=1, source_target_pairs={{0,192},{64,0},{128,64},{192,128},{1,193},{65,1},{129,65},{193,129... | collective-permute-start | bytes 491528 | tf_op jit(solution)/shard_map/ppermute | solution.py:19
  44.3 2.6 %collective-permute-done.8 = bf16[128,640]{1,0:T(8,128)(2,1)S(1)} collective-permute-done((bf16[128,640]{1,0:T(8,128)(2,1)S(1)}, bf16[128,640]{1,0:T(8,128)(2,1)S(1)}, u32[]{:S(2)}, u32[]{:S(2)}) %collective-permute-start.8) | collective-permute-done | bytes 163872 | tf_op jit(solution)/shard_map/ppermute | solution.py:19
  47.6 3.4 %product.2 = f32[501,640]{1,0:T(8,128)S(1)} custom-call(bf16[501,2048]{1,0:T(8,128)(2,1)} %collective-permute-done.weight_ref.other_ref, bf16[1024,640]{1,0:T(8,128)(2,1)S(1)} %bitcast.144, bf16[1024,640]{1,0:T(8,128)(2,1)S(1)} %bitcast.146), custom_call_target="tpu_custom_call" | custom-call | flops 1313341440 | bytes 6291456 | tf_op jit(solution)/shard_map/product/pallas_call | solution.py:195
  57.3 11.4 %all-to-all-start.1 = ((f32[32,8,128]{2,1,0:T(8,128)}), f32[32,8,128]{2,1,0:T(8,128)S(1)}, u32[]{:S(2)}, u32[]{:S(2)}) async-start(f32[32,8,128]{2,1,0:T(8,128)} %broadcast_in_dim.85), calls=%async_computation.1 | async-start | bytes 262144 | tf_op jit(solution)/shard_map/all_to_all | solution.py:66
  68.7 9.0 %all-to-all-done.1 = f32[32,8,128]{2,1,0:T(8,128)S(1)} async-done(((f32[32,8,128]{2,1,0:T(8,128)}), f32[32,8,128]{2,1,0:T(8,128)S(1)}, u32[]{:S(2)}, u32[]{:S(2)}) %all-to-all-start.1) | async-done | bytes 131104 | tf_op jit(solution)/shard_map/all_to_all | solution.py:66
  77.9 9.8 %all_to_all.25 = f32[8,8,128]{2,1,0:T(8,128)S(1)} all-to-all(f32[8,8,128]{2,1,0:T(8,128)S(1)} %broadcast_in_dim.86), channel_id=1, replica_groups=mesh['x'=4,'c'=2,'z'=8,'y'=4] {'x','c'}, dimensions={0} | all-to-all | bytes 65536 | tf_op jit(solution)/shard_map/all_to_all | solution.py:66
  92.4 6.5 %pull.1 = f32[2048,640]{1,0:T(8,128)S(1)} custom-call(bf16[501,2048]{1,0:T(8,128)(2,1)S(1)} %get-tuple-element.37.weight_ref.mine_ref, bf16[501,2048]{1,0:T(8,128)(2,1)} %collective-permute-done.weight_ref.other_ref, bf16[501,640]{1,0:T(8,128)(2,1)S(1)} %logit_grad.1.grad_ref, bf16[501,640]{1,0:T(8,128)(2,1)S(1)} %collective-permute-done.10.other_grad_ref), custom_call_target="tpu_custom_call" | custom-call | flops 2626682880 | bytes 12582912 | tf_op jit(solution)/shard_map/pull/pallas_call | solution.py:219
  100.0 2.7 %collective-permute-start.13 = (f16[128,640]{1,0:T(8,128)(2,1)S(1)}, f16[128,640]{1,0:T(8,128)(2,1)S(1)}, u32[]{:S(2)}, u32[]{:S(2)}) collective-permute-start(f16[128,640]{1,0:T(8,128)(2,1)S(1)} %get-tuple-element.53), channel_id=1, source_target_pairs={{0,192},{64,0},{128,64},{192,128},{1,193},{65,1},{129,65},{193,129... | collective-permute-start | bytes 491528 | tf_op jit(solution)/shard_map/ppermute | solution.py:19
  107.3 3.3 %collective-permute-start.14 = (f16[256,640]{1,0:T(8,128)(2,1)S(1)}, f16[256,640]{1,0:T(8,128)(2,1)S(1)}, u32[]{:S(2)}, u32[]{:S(2)}) collective-permute-start(f16[256,640]{1,0:T(8,128)(2,1)S(1)} %pad_maximum_fusion.1), channel_id=1, source_target_pairs={{0,192},{64,0},{128,64},{192,128},{1,193},{65,1},{129,65},{193,129... | collective-permute-start | bytes 983048 | tf_op jit(solution)/shard_map/ppermute | solution.py:19
  114.0 3.3 %collective-permute-done.12 = f16[256,640]{1,0:T(8,128)(2,1)S(1)} collective-permute-done((f16[256,640]{1,0:T(8,128)(2,1)S(1)}, f16[256,640]{1,0:T(8,128)(2,1)S(1)}, u32[]{:S(2)}, u32[]{:S(2)}) %collective-permute-start.12) | collective-permute-done | bytes 327712 | tf_op jit(solution)/shard_map/ppermute | solution.py:19
  121.0 2.7 %collective-permute-done.21 = f16[256,640]{1,0:T(8,128)(2,1)S(1)} collective-permute-done((f16[256,640]{1,0:T(8,128)(2,1)S(1)}, f16[256,640]{1,0:T(8,128)(2,1)S(1)}, u32[]{:S(2)}, u32[]{:S(2)}) %collective-permute-start.21) | collective-permute-done | bytes 327712 | tf_op jit(solution)/shard_map/ppermute | solution.py:19
  127.2 3.2 %collective-permute-done.22 = f16[64,640]{1,0:T(8,128)(2,1)S(1)} collective-permute-done((f16[64,640]{1,0:T(8,128)(2,1)S(1)}, f16[64,640]{1,0:T(8,128)(2,1)S(1)}, u32[]{:S(2)}, u32[]{:S(2)}) %collective-permute-start.22) | collective-permute-done | bytes 81952 | tf_op jit(solution)/shard_map/ppermute | solution.py:19
  133.2 18.3 %all_to_all.26 = f16[64,16,128]{2,1,0:T(8,128)(2,1)S(1)} all-to-all(f16[64,16,128]{2,1,0:T(8,128)(2,1)S(1)} %bitcast.170), channel_id=1, replica_groups=mesh['x'=4,'c'=2,'z'=8,'y'=4] {'x','c','z'}, dimensions={0} | all-to-all | bytes 524288 | tf_op jit(solution)/shard_map/all_to_all | solution.py:66
  151.6 14.7 %all_to_all.27 = f16[8,128,128]{2,1,0:T(8,128)(2,1)S(1)} all-to-all(f16[8,128,128]{2,1,0:T(8,128)(2,1)S(1)} %broadcast_in_dim.88), channel_id=1, replica_groups=mesh['x'=4,'c'=2,'z'=8,'y'=4] {'z'}, dimensions={0} | all-to-all | bytes 524288 | tf_op jit(solution)/shard_map/all_to_all | solution.py:66
  175.4 2.7 %collective-permute-done.27 = f16[512,128]{1,0:T(8,128)(2,1)S(1)} collective-permute-done((f16[512,128]{1,0:T(8,128)(2,1)S(1)}, f16[512,128]{1,0:T(8,128)(2,1)S(1)}, u32[]{:S(2)}, u32[]{:S(2)}) %collective-permute-start.27) | collective-permute-done | bytes 131104 | tf_op jit(solution)/shard_map/ppermute | solution.py:19
  178.0 3.4 %collective-permute-done.28 = f16[512,128]{1,0:T(8,128)(2,1)S(1)} collective-permute-done((f16[512,128]{1,0:T(8,128)(2,1)S(1)}, f16[512,128]{1,0:T(8,128)(2,1)S(1)}, u32[]{:S(2)}, u32[]{:S(2)}) %collective-permute-start.28) | collective-permute-done | bytes 131104 | tf_op jit(solution)/shard_map/ppermute | solution.py:19
  182.9 3.0 %shard_map.95 = bf16[128,4096]{1,0:T(8,128)(2,1)} custom-call(f32[4,8,4,2,2,8,128]{6,5,4,3,2,1,0:T(8,128)S(1)} %convert.43.grad_ref, bf16[128,4096]{1,0:T(8,128)(2,1)S(1)} %bitcast.149, f32[1,4096]{1,0:T(1,128)S(1)} %bitcast.151), custom_call_target="tpu_custom_call" | custom-call | flops 4194304 | bytes 4194304 | tf_op jit(solution)/shard_map/pallas_call | solution.py:311
  (120 shorter events, 45.4 us)
Async XLA Ops:
  4.3 20.6 %all-to-all-start = ((bf16[8,528,128]{2,1,0:T(8,128)(2,1)}), bf16[8,528,128]{2,1,0:T(8,128)(2,1)S(1)}, u32[]{:S(2)}, u32[]{:S(2)}) async-start(bf16[8,528,128]{2,1,0:T(8,128)(2,1)} %normed_slices.1), calls=%async_computation | async-start | bytes 2162688 | tf_op jit(solution)/shard_map/all_to_all | solution.py:66
  12.5 35.0 %collective-permute-start = (bf16[501,2048]{1,0:T(8,128)(2,1)}, bf16[501,2048]{1,0:T(8,128)(2,1)}, u32[]{:S(2)}, u32[]{:S(2)}) collective-permute-start(bf16[501,2048]{1,0:T(8,128)(2,1)} %get-tuple-element.36), channel_id=1, source_target_pairs={{0,32},{32,0},{1,33},{33,1},{2,34},{34,2},{3,35},{35,3},{4,36},{36... | collective-permute-start | bytes 6156296 | tf_op jit(solution)/shard_map/ppermute | solution.py:23
  26.7 13.6 %collective-permute-start.5 = (bf16[256,640]{1,0:T(8,128)(2,1)S(1)}, bf16[256,640]{1,0:T(8,128)(2,1)S(1)}, u32[]{:S(2)}, u32[]{:S(2)}) collective-permute-start(bf16[256,640]{1,0:T(8,128)(2,1)S(1)} %get-tuple-element.19), channel_id=1, source_target_pairs={{0,3},{1,0},{2,1},{3,2},{4,7},{5,4},{6,5},{7,6},{8,11},{9,8},{10,9... | collective-permute-start | bytes 983048 | tf_op jit(solution)/shard_map/ppermute | solution.py:19
  27.5 9.0 %collective-permute-start.6 = (bf16[256,640]{1,0:T(8,128)(2,1)S(1)}, bf16[256,640]{1,0:T(8,128)(2,1)S(1)}, u32[]{:S(2)}, u32[]{:S(2)}) collective-permute-start(bf16[256,640]{1,0:T(8,128)(2,1)S(1)} %get-tuple-element.19), channel_id=1, source_target_pairs={{0,1},{1,2},{2,3},{3,0},{4,5},{5,6},{6,7},{7,4},{8,9},{9,10},{10,1... | collective-permute-start | bytes 983048 | tf_op jit(solution)/shard_map/ppermute | solution.py:19
  30.0 11.1 %collective-permute-start.1 = (bf16[256,640]{1,0:T(8,128)(2,1)S(1)}, bf16[256,640]{1,0:T(8,128)(2,1)S(1)}, u32[]{:S(2)}, u32[]{:S(2)}) collective-permute-start(bf16[256,640]{1,0:T(8,128)(2,1)S(1)} %get-tuple-element.18), channel_id=1, source_target_pairs={{0,192},{64,0},{128,64},{192,128},{1,193},{65,1},{129,65},{193,129... | collective-permute-start | bytes 983048 | tf_op jit(solution)/shard_map/ppermute | solution.py:19
  31.1 9.6 %collective-permute-start.2 = (bf16[256,640]{1,0:T(8,128)(2,1)S(1)}, bf16[256,640]{1,0:T(8,128)(2,1)S(1)}, u32[]{:S(2)}, u32[]{:S(2)}) collective-permute-start(bf16[256,640]{1,0:T(8,128)(2,1)S(1)} %get-tuple-element.18), channel_id=1, source_target_pairs={{0,64},{64,128},{128,192},{192,0},{1,65},{65,129},{129,193},{193,1... | collective-permute-start | bytes 983048 | tf_op jit(solution)/shard_map/ppermute | solution.py:19
  36.5 7.8 %collective-permute-start.7 = (bf16[128,640]{1,0:T(8,128)(2,1)S(1)}, bf16[128,640]{1,0:T(8,128)(2,1)S(1)}, u32[]{:S(2)}, u32[]{:S(2)}) collective-permute-start(bf16[128,640]{1,0:T(8,128)(2,1)S(1)} %slice.146), channel_id=1, source_target_pairs={{0,1},{1,2},{2,3},{3,0},{4,5},{5,6},{6,7},{7,4},{8,9},{9,10},{10,1... | collective-permute-start | bytes 491528 | tf_op jit(solution)/shard_map/ppermute | solution.py:19
  40.3 6.6 %collective-permute-start.8 = (bf16[128,640]{1,0:T(8,128)(2,1)S(1)}, bf16[128,640]{1,0:T(8,128)(2,1)S(1)}, u32[]{:S(2)}, u32[]{:S(2)}) collective-permute-start(bf16[128,640]{1,0:T(8,128)(2,1)S(1)} %slice.147), channel_id=1, source_target_pairs={{0,3},{1,0},{2,1},{3,2},{4,7},{5,4},{6,5},{7,6},{8,11},{9,8},{10,9... | collective-permute-start | bytes 491528 | tf_op jit(solution)/shard_map/ppermute | solution.py:19
  40.8 6.6 %collective-permute-start.3 = (bf16[128,640]{1,0:T(8,128)(2,1)S(1)}, bf16[128,640]{1,0:T(8,128)(2,1)S(1)}, u32[]{:S(2)}, u32[]{:S(2)}) collective-permute-start(bf16[128,640]{1,0:T(8,128)(2,1)S(1)} %slice.144), channel_id=1, source_target_pairs={{0,64},{64,128},{128,192},{192,0},{1,65},{65,129},{129,193},{193,1... | collective-permute-start | bytes 491528 | tf_op jit(solution)/shard_map/ppermute | solution.py:19
  57.3 20.5 %all-to-all-start.1 = ((f32[32,8,128]{2,1,0:T(8,128)}), f32[32,8,128]{2,1,0:T(8,128)S(1)}, u32[]{:S(2)}, u32[]{:S(2)}) async-start(f32[32,8,128]{2,1,0:T(8,128)} %broadcast_in_dim.85), calls=%async_computation.1 | async-start | bytes 262144 | tf_op jit(solution)/shard_map/all_to_all | solution.py:66
  99.4 7.5 %collective-permute-start.11 = (f16[128,640]{1,0:T(8,128)(2,1)S(1)}, f16[128,640]{1,0:T(8,128)(2,1)S(1)}, u32[]{:S(2)}, u32[]{:S(2)}) collective-permute-start(f16[128,640]{1,0:T(8,128)(2,1)S(1)} %get-tuple-element.52), channel_id=1, source_target_pairs={{0,64},{64,128},{128,192},{192,0},{1,65},{65,129},{129,193},{193,1... | collective-permute-start | bytes 491528 | tf_op jit(solution)/shard_map/ppermute | solution.py:19
  100.0 6.9 %collective-permute-start.13 = (f16[128,640]{1,0:T(8,128)(2,1)S(1)}, f16[128,640]{1,0:T(8,128)(2,1)S(1)}, u32[]{:S(2)}, u32[]{:S(2)}) collective-permute-start(f16[128,640]{1,0:T(8,128)(2,1)S(1)} %get-tuple-element.53), channel_id=1, source_target_pairs={{0,192},{64,0},{128,64},{192,128},{1,193},{65,1},{129,65},{193,129... | collective-permute-start | bytes 491528 | tf_op jit(solution)/shard_map/ppermute | solution.py:19
  102.9 7.7 %collective-permute-start.18 = (f16[128,640]{1,0:T(8,128)(2,1)S(1)}, f16[128,640]{1,0:T(8,128)(2,1)S(1)}, u32[]{:S(2)}, u32[]{:S(2)}) collective-permute-start(f16[128,640]{1,0:T(8,128)(2,1)S(1)} %get-tuple-element.54), channel_id=1, source_target_pairs={{0,1},{1,2},{2,3},{3,0},{4,5},{5,6},{6,7},{7,4},{8,9},{9,10},{10,1... | collective-permute-start | bytes 491528 | tf_op jit(solution)/shard_map/ppermute | solution.py:19
  104.9 6.6 %collective-permute-start.20 = (f16[128,640]{1,0:T(8,128)(2,1)S(1)}, f16[128,640]{1,0:T(8,128)(2,1)S(1)}, u32[]{:S(2)}, u32[]{:S(2)}) collective-permute-start(f16[128,640]{1,0:T(8,128)(2,1)S(1)} %get-tuple-element.55), channel_id=1, source_target_pairs={{0,3},{1,0},{2,1},{3,2},{4,7},{5,4},{6,5},{7,6},{8,11},{9,8},{10,9... | collective-permute-start | bytes 491528 | tf_op jit(solution)/shard_map/ppermute | solution.py:19
  107.1 10.2 %collective-permute-start.12 = (f16[256,640]{1,0:T(8,128)(2,1)S(1)}, f16[256,640]{1,0:T(8,128)(2,1)S(1)}, u32[]{:S(2)}, u32[]{:S(2)}) collective-permute-start(f16[256,640]{1,0:T(8,128)(2,1)S(1)} %pad_maximum_fusion), channel_id=1, source_target_pairs={{0,64},{64,128},{128,192},{192,0},{1,65},{65,129},{129,193},{193,1... | collective-permute-start | bytes 983048 | tf_op jit(solution)/shard_map/ppermute | solution.py:19
  107.3 10.0 %collective-permute-start.14 = (f16[256,640]{1,0:T(8,128)(2,1)S(1)}, f16[256,640]{1,0:T(8,128)(2,1)S(1)}, u32[]{:S(2)}, u32[]{:S(2)}) collective-permute-start(f16[256,640]{1,0:T(8,128)(2,1)S(1)} %pad_maximum_fusion.1), channel_id=1, source_target_pairs={{0,192},{64,0},{128,64},{192,128},{1,193},{65,1},{129,65},{193,129... | collective-permute-start | bytes 983048 | tf_op jit(solution)/shard_map/ppermute | solution.py:19
  111.7 9.2 %collective-permute-start.19 = (f16[256,640]{1,0:T(8,128)(2,1)S(1)}, f16[256,640]{1,0:T(8,128)(2,1)S(1)}, u32[]{:S(2)}, u32[]{:S(2)}) collective-permute-start(f16[256,640]{1,0:T(8,128)(2,1)S(1)} %pad_maximum_fusion.2), channel_id=1, source_target_pairs={{0,1},{1,2},{2,3},{3,0},{4,5},{5,6},{6,7},{7,4},{8,9},{9,10},{10,1... | collective-permute-start | bytes 983048 | tf_op jit(solution)/shard_map/ppermute | solution.py:19
  112.9 10.7 %collective-permute-start.21 = (f16[256,640]{1,0:T(8,128)(2,1)S(1)}, f16[256,640]{1,0:T(8,128)(2,1)S(1)}, u32[]{:S(2)}, u32[]{:S(2)}) collective-permute-start(f16[256,640]{1,0:T(8,128)(2,1)S(1)} %pad_maximum_fusion.3), channel_id=1, source_target_pairs={{0,3},{1,0},{2,1},{3,2},{4,7},{5,4},{6,5},{7,6},{8,11},{9,8},{10,9... | collective-permute-start | bytes 983048 | tf_op jit(solution)/shard_map/ppermute | solution.py:19
  117.5 8.1 %collective-permute-start.15 = (f16[64,640]{1,0:T(8,128)(2,1)S(1)}, f16[64,640]{1,0:T(8,128)(2,1)S(1)}, u32[]{:S(2)}, u32[]{:S(2)}) collective-permute-start(f16[64,640]{1,0:T(8,128)(2,1)S(1)} %get-tuple-element.46), channel_id=1, source_target_pairs={{0,1},{1,2},{2,3},{3,0},{4,5},{5,6},{6,7},{7,4},{8,9},{9,10},{10,1... | collective-permute-start | bytes 245768 | tf_op jit(solution)/shard_map/ppermute | solution.py:19
  119.6 7.6 %collective-permute-start.16 = (f16[64,640]{1,0:T(8,128)(2,1)S(1)}, f16[64,640]{1,0:T(8,128)(2,1)S(1)}, u32[]{:S(2)}, u32[]{:S(2)}) collective-permute-start(f16[64,640]{1,0:T(8,128)(2,1)S(1)} %get-tuple-element.48), channel_id=1, source_target_pairs={{0,2},{1,3},{2,0},{3,1},{4,6},{5,7},{6,4},{7,5},{8,10},{9,11},{10,... | collective-permute-start | bytes 245768 | tf_op jit(solution)/shard_map/ppermute | solution.py:19
  120.2 7.0 %collective-permute-start.17 = (f16[64,640]{1,0:T(8,128)(2,1)S(1)}, f16[64,640]{1,0:T(8,128)(2,1)S(1)}, u32[]{:S(2)}, u32[]{:S(2)}) collective-permute-start(f16[64,640]{1,0:T(8,128)(2,1)S(1)} %get-tuple-element.47), channel_id=1, source_target_pairs={{0,3},{1,0},{2,1},{3,2},{4,7},{5,4},{6,5},{7,6},{8,11},{9,8},{10,9... | collective-permute-start | bytes 245768 | tf_op jit(solution)/shard_map/ppermute | solution.py:19
  123.8 6.6 %collective-permute-start.22 = (f16[64,640]{1,0:T(8,128)(2,1)S(1)}, f16[64,640]{1,0:T(8,128)(2,1)S(1)}, u32[]{:S(2)}, u32[]{:S(2)}) collective-permute-start(f16[64,640]{1,0:T(8,128)(2,1)S(1)} %get-tuple-element.49), channel_id=1, source_target_pairs={{0,64},{64,128},{128,192},{192,0},{1,65},{65,129},{129,193},{193,1... | collective-permute-start | bytes 245768 | tf_op jit(solution)/shard_map/ppermute | solution.py:19
  166.4 6.6 %collective-permute-start.26 = (f16[1024,128]{1,0:T(8,128)(2,1)S(1)}, f16[1024,128]{1,0:T(8,128)(2,1)S(1)}, u32[]{:S(2)}, u32[]{:S(2)}) collective-permute-start(f16[1024,128]{1,0:T(8,128)(2,1)S(1)} %bitcast.166), channel_id=1, source_target_pairs={{0,1},{1,2},{2,3},{3,0},{4,5},{5,6},{6,7},{7,4},{8,9},{9,10},{10,1... | collective-permute-start | bytes 786440 | tf_op jit(solution)/shard_map/ppermute | solution.py:19
  167.5 7.7 %collective-permute-start.25 = (f16[1024,128]{1,0:T(8,128)(2,1)S(1)}, f16[1024,128]{1,0:T(8,128)(2,1)S(1)}, u32[]{:S(2)}, u32[]{:S(2)}) collective-permute-start(f16[1024,128]{1,0:T(8,128)(2,1)S(1)} %bitcast.167), channel_id=1, source_target_pairs={{0,3},{1,0},{2,1},{3,2},{4,7},{5,4},{6,5},{7,6},{8,11},{9,8},{10,9... | collective-permute-start | bytes 786440 | tf_op jit(solution)/shard_map/ppermute | solution.py:19
  (12 other events, 56.5 us)
where the time goes:
time: 188 us; the launch traced here: 187 us
  starting transfers between devices  51 us (27%)
  waiting for transfers between devices  51 us (27%)
  blocking collectives  42.9 us (23%)
  Pallas kernels  21.8 us (12%)
  local copies, waits for them, and re-layouts  10.7 us (6%)
  between operations  4.82 us (3%)
  other arithmetic  3.15 us (2%)
    all_to_all x3, blocking collectives, exchange(): return lax.all_to_all(value, axes, 0, 0)  42.9 us
    ppermute x26, starting transfers between devices, shift(): return lax.ppermute(value, axis, [(i, (i + by) % n) for i in range(n)])  34.4 us
    ppermute x26, waiting for transfers between devices, shift(): return lax.ppermute(value, axis, [(i, (i + by) % n) for i in range(n)])  28.1 us
    all_to_all x2, waiting for transfers between devices, exchange(): return lax.all_to_all(value, axes, 0, 0)  20.2 us
    all_to_all x2, starting transfers between devices, exchange(): return lax.all_to_all(value, axes, 0, 0)  15.7 us
    pallas_call x1, Pallas kernels, pull(): pl.pallas_call(pull_kernel, name='pull', out_shape=jax.ShapeDtypeStruct((...  6.53 us
    pallas_call x2, Pallas kernels, product(): pl.pallas_call(product_kernel, name='product', out_shape=jax.ShapeDtypeSt...  5.21 us
    dynamic_slice x1, local copies, waits for them, and re-layouts, body(): lax.dynamic_slice_in_dim(late_weight, (1 - core) * half, half, 1)  3.94 us
  transfers between devices with their start and end apart: 31, of which 18 were waited for; matrix products, arithmetic and copies ran while one was open for 4% of the time, Pallas kernels for 2%

commit v1 on v0

--- a/solution.py
+++ b/solution.py
@@ -100,7 +100,7 @@
 
     def tile(offset):
         at = pl.ds(pl.multiple_of(offset, 128), 128)
-        return (h_ref[:, at].astype(F32) * scales[...] * gain_ref[:, at]).T.astype(BF16)
+        return (h_ref[:, at].astype(F32) * scales[...] * gain_ref[:, at]).astype(BF16).T
 
     word = target_ref[...]
     rows = [word & 255, (word >> 8) & 255, word >> 16, mask_ref[...], position_ref[...]]
@@ -205,13 +205,13 @@
 
 def pull_kernel(mine_ref, other_ref, grad_ref, other_grad_ref, out_ref):
     def step(i, carry):
-        at = pl.ds(pl.multiple_of(i * 256, 256), 256)
+        at = pl.ds(pl.multiple_of(i * 512, 512), 512)
         out_ref[at, :] = lax.dot_general(
             mine_ref[:, at], grad_ref[...], TN, preferred_element_type=F32
         ) + lax.dot_general(other_ref[:, at], other_grad_ref[...], TN, preferred_element_type=F32)
         return carry
 
-    lax.fori_loop(0, out_ref.shape[0] // 256, step, 0)
+    lax.fori_loop(0, out_ref.shape[0] // 512, step, 0)
 
 
 def pull(mine, other, grad, other_grad):
@@ -348,8 +348,8 @@
     sib = product(other, one, two)
     sib, one, two = lax.optimization_barrier((sib, one, two))
     logits, stats = stats_of(weight_total.reshape(1), product(mine, one, two), swap_cores(sib), word)
-    stats = merge_rows(everyone(stats, ("z", "y")))
-    stats = merge_rows(everyone(stats, PIPE))
+    stats = merge_rows(everyone(stats, ("z",)))
+    stats = merge_rows(everyone(stats, ("x", "c", "y")))
     weight = (jnp.arange(8 * slots, dtype=F32).reshape(8, slots) < weight_total).astype(F32)
     loss = (jnp.sum((weight * stats)[:5]) - stats[5, 0]) / weight_total
     logit_grad = grad_of(logits, stats, coef, word)

time: 188 us -> 186 us (0.989)
  blocking collectives: 42.9 us -> 46.2 us
  starting transfers between devices: 51 us -> 49 us
  waiting for transfers between devices: 51 us -> 49 us
    all_to_all x3, blocking collectives: 42.9 us -> 46.2 us  [exchange(): return lax.all_to_all(value, axes, 0, 0)]
    all_to_all x2, starting transfers between devices: 15.7 us -> 12.8 us  [exchange(): return lax.all_to_all(value, axes, 0, 0)]
  transfers between devices with their start and end apart: 31 -> 31, of which waited for: 18 -> 17; matrix products, arithmetic and copies ran while one was open for 4% -> 4% of each run, Pallas kernels for 2% -> 2%
where the time goes in v1:
time: 186 us; the launch traced here: 185 us
  starting transfers between devices  49 us (26%)
  waiting for transfers between devices  49 us (26%)
  blocking collectives  46.2 us (25%)
  Pallas kernels  20.9 us (11%)
  local copies, waits for them, and re-layouts  10.6 us (6%)
  between operations  4.81 us (3%)
  other arithmetic  3.15 us (2%)
    all_to_all x3, blocking collectives, exchange(): return lax.all_to_all(value, axes, 0, 0)  46.2 us
    ppermute x26, starting transfers between devices, shift(): return lax.ppermute(value, axis, [(i, (i + by) % n) for i in range(n)])  35.4 us
    ppermute x26, waiting for transfers between devices, shift(): return lax.ppermute(value, axis, [(i, (i + by) % n) for i in range(n)])  27.1 us
    all_to_all x2, waiting for transfers between devices, exchange(): return lax.all_to_all(value, axes, 0, 0)  19.2 us
    all_to_all x2, starting transfers between devices, exchange(): return lax.all_to_all(value, axes, 0, 0)  12.8 us
    pallas_call x1, Pallas kernels, pull(): pl.pallas_call(pull_kernel, name='pull', out_shape=jax.ShapeDtypeStruct((...  5.67 us
    pallas_call x2, Pallas kernels, product(): pl.pallas_call(product_kernel, name='product', out_shape=jax.ShapeDtypeSt...  5.21 us
    dynamic_slice x1, local copies, waits for them, and re-layouts, body(): lax.dynamic_slice_in_dim(late_weight, (1 - core) * half, half, 1)  3.94 us
  transfers between devices with their start and end apart: 31, of which 17 were waited for; matrix products, arithmetic and copies ran while one was open for 4% of the time, Pallas kernels for 2%

profile of v1, /device:TPU:24, one launch (start us, length us, event | category | flops | bytes accessed | tf_op | source)
XLA Modules:
  0.0 185.3 jit_solution(18150135603220836452)
XLA Ops:
  0.6 3.6 %normed_slices.1 = bf16[8,528,128]{2,1,0:T(8,128)(2,1)} custom-call(s32[1]{0:T(128)} %bitcast.2.y_ref, bf16[128,4096]{1,0:T(8,128)(2,1)} %bitcast.148, f32[1,4096]{1,0:T(1,128)} %bitcast.150, s32[1,128]{1,0:T(1,128)} %target_ref.1, s32[1,128]{1,0:T(1,128)} %mask_ref.1, s32[1,128]{1,0:T(1,128)} %position_ref.1), custom_call_target="tpu_custom_call" | custom-call | flops 2097152 | bytes 2097152 | tf_op jit(solution)/shard_map/normed_slices/pallas_call | solution.py:124
  4.2 4.3 %all-to-all-start = ((bf16[8,528,128]{2,1,0:T(8,128)(2,1)}), bf16[8,528,128]{2,1,0:T(8,128)(2,1)S(1)}, u32[]{:S(2)}, u32[]{:S(2)}) async-start(bf16[8,528,128]{2,1,0:T(8,128)(2,1)} %normed_slices.1), calls=%async_computation | async-start | bytes 2162688 | tf_op jit(solution)/shard_map/all_to_all | solution.py:66
  8.5 3.9 %constant_dynamic-slice_fusion = (bf16[501,2048]{1,0:T(8,128)(2,1)}, bf16[501,2048]{1,0:T(8,128)(2,1)S(1)}) fusion(bf16[501,4096]{1,0:T(8,128)(2,1)} %param.10, s32[]{:T(128)S(6)} %select_n.141, s32[]{:T(128)S(6)} %select_n.140), kind=kLoop, calls=%fused_computation.78 | loop fusion | bytes 8208392 | tf_op jit(solution)/shard_map/dynamic_slice | solution.py:339
  13.6 11.2 %all-to-all-done.packed_ref = bf16[8,528,128]{2,1,0:T(8,128)(2,1)S(1)} async-done(((bf16[8,528,128]{2,1,0:T(8,128)(2,1)}), bf16[8,528,128]{2,1,0:T(8,128)(2,1)S(1)}, u32[]{:S(2)}, u32[]{:S(2)}) %all-to-all-start) | async-done | bytes 1081376 | tf_op jit(solution)/shard_map/all_to_all | solution.py:66
  27.4 2.5 %collective-permute-start.6 = (bf16[256,640]{1,0:T(8,128)(2,1)S(1)}, bf16[256,640]{1,0:T(8,128)(2,1)S(1)}, u32[]{:S(2)}, u32[]{:S(2)}) collective-permute-start(bf16[256,640]{1,0:T(8,128)(2,1)S(1)} %get-tuple-element.19), channel_id=1, source_target_pairs={{0,1},{1,2},{2,3},{3,0},{4,5},{5,6},{6,7},{7,4},{8,9},{9,10},{10,1... | collective-permute-start | bytes 983048 | tf_op jit(solution)/shard_map/ppermute | solution.py:19
  32.2 4.1 %collective-permute-done.6 = bf16[256,640]{1,0:T(8,128)(2,1)S(1)} collective-permute-done((bf16[256,640]{1,0:T(8,128)(2,1)S(1)}, bf16[256,640]{1,0:T(8,128)(2,1)S(1)}, u32[]{:S(2)}, u32[]{:S(2)}) %collective-permute-start.6) | collective-permute-done | bytes 327712 | tf_op jit(solution)/shard_map/ppermute | solution.py:19
  36.4 3.8 %collective-permute-start.7 = (bf16[128,640]{1,0:T(8,128)(2,1)S(1)}, bf16[128,640]{1,0:T(8,128)(2,1)S(1)}, u32[]{:S(2)}, u32[]{:S(2)}) collective-permute-start(bf16[128,640]{1,0:T(8,128)(2,1)S(1)} %slice.146), channel_id=1, source_target_pairs={{0,1},{1,2},{2,3},{3,0},{4,5},{5,6},{6,7},{7,4},{8,9},{9,10},{10,1... | collective-permute-start | bytes 491528 | tf_op jit(solution)/shard_map/ppermute | solution.py:19
  41.0 3.1 %collective-permute-start.4 = (bf16[128,640]{1,0:T(8,128)(2,1)S(1)}, bf16[128,640]{1,0:T(8,128)(2,1)S(1)}, u32[]{:S(2)}, u32[]{:S(2)}) collective-permute-start(bf16[128,640]{1,0:T(8,128)(2,1)S(1)} %slice.145), channel_id=1, source_target_pairs={{0,192},{64,0},{128,64},{192,128},{1,193},{65,1},{129,65},{193,129... | collective-permute-start | bytes 491528 | tf_op jit(solution)/shard_map/ppermute | solution.py:19
  44.2 2.6 %collective-permute-done.8 = bf16[128,640]{1,0:T(8,128)(2,1)S(1)} collective-permute-done((bf16[128,640]{1,0:T(8,128)(2,1)S(1)}, bf16[128,640]{1,0:T(8,128)(2,1)S(1)}, u32[]{:S(2)}, u32[]{:S(2)}) %collective-permute-start.8) | collective-permute-done | bytes 163872 | tf_op jit(solution)/shard_map/ppermute | solution.py:19
  47.5 3.4 %product.2 = f32[501,640]{1,0:T(8,128)S(1)} custom-call(bf16[501,2048]{1,0:T(8,128)(2,1)} %collective-permute-done.weight_ref.other_ref, bf16[1024,640]{1,0:T(8,128)(2,1)S(1)} %bitcast.144, bf16[1024,640]{1,0:T(8,128)(2,1)S(1)} %bitcast.146), custom_call_target="tpu_custom_call" | custom-call | flops 1313341440 | bytes 6291456 | tf_op jit(solution)/shard_map/product/pallas_call | solution.py:195
  57.2 8.5 %all-to-all-start.1 = ((f32[8,8,128]{2,1,0:T(8,128)}), f32[8,8,128]{2,1,0:T(8,128)S(1)}, u32[]{:S(2)}, u32[]{:S(2)}) async-start(f32[8,8,128]{2,1,0:T(8,128)} %broadcast_in_dim.85), calls=%async_computation.1 | async-start | bytes 65536 | tf_op jit(solution)/shard_map/all_to_all | solution.py:66
  65.6 8.0 %all-to-all-done.1 = f32[8,8,128]{2,1,0:T(8,128)S(1)} async-done(((f32[8,8,128]{2,1,0:T(8,128)}), f32[8,8,128]{2,1,0:T(8,128)S(1)}, u32[]{:S(2)}, u32[]{:S(2)}) %all-to-all-start.1) | async-done | bytes 32800 | tf_op jit(solution)/shard_map/all_to_all | solution.py:66
  73.8 13.6 %all_to_all.25 = f32[32,8,128]{2,1,0:T(8,128)S(1)} all-to-all(f32[32,8,128]{2,1,0:T(8,128)S(1)} %broadcast_in_dim.86), channel_id=1, replica_groups=mesh['x'=4,'c'=2,'z'=8,'y'=4] {'x','c','y'}, dimensions={0} | all-to-all | bytes 262144 | tf_op jit(solution)/shard_map/all_to_all | solution.py:66
  92.0 5.7 %pull.1 = f32[2048,640]{1,0:T(8,128)S(1)} custom-call(bf16[501,2048]{1,0:T(8,128)(2,1)S(1)} %get-tuple-element.37.weight_ref.mine_ref, bf16[501,2048]{1,0:T(8,128)(2,1)} %collective-permute-done.weight_ref.other_ref, bf16[501,640]{1,0:T(8,128)(2,1)S(1)} %logit_grad.1.grad_ref, bf16[501,640]{1,0:T(8,128)(2,1)S(1)} %collective-permute-done.10.other_grad_ref), custom_call_target="tpu_custom_call" | custom-call | flops 2626682880 | bytes 12582912 | tf_op jit(solution)/shard_map/pull/pallas_call | solution.py:219
  98.9 2.6 %collective-permute-start.13 = (f16[128,640]{1,0:T(8,128)(2,1)S(1)}, f16[128,640]{1,0:T(8,128)(2,1)S(1)}, u32[]{:S(2)}, u32[]{:S(2)}) collective-permute-start(f16[128,640]{1,0:T(8,128)(2,1)S(1)} %get-tuple-element.53), channel_id=1, source_target_pairs={{0,192},{64,0},{128,64},{192,128},{1,193},{65,1},{129,65},{193,129... | collective-permute-start | bytes 491528 | tf_op jit(solution)/shard_map/ppermute | solution.py:19
  106.1 3.3 %collective-permute-start.14 = (f16[256,640]{1,0:T(8,128)(2,1)S(1)}, f16[256,640]{1,0:T(8,128)(2,1)S(1)}, u32[]{:S(2)}, u32[]{:S(2)}) collective-permute-start(f16[256,640]{1,0:T(8,128)(2,1)S(1)} %pad_maximum_fusion.1), channel_id=1, source_target_pairs={{0,192},{64,0},{128,64},{192,128},{1,193},{65,1},{129,65},{193,129... | collective-permute-start | bytes 983048 | tf_op jit(solution)/shard_map/ppermute | solution.py:19
  112.6 3.4 %collective-permute-done.12 = f16[256,640]{1,0:T(8,128)(2,1)S(1)} collective-permute-done((f16[256,640]{1,0:T(8,128)(2,1)S(1)}, f16[256,640]{1,0:T(8,128)(2,1)S(1)}, u32[]{:S(2)}, u32[]{:S(2)}) %collective-permute-start.12) | collective-permute-done | bytes 327712 | tf_op jit(solution)/shard_map/ppermute | solution.py:19
  122.3 2.5 %collective-permute-start.23 = (f16[64,640]{1,0:T(8,128)(2,1)S(1)}, f16[64,640]{1,0:T(8,128)(2,1)S(1)}, u32[]{:S(2)}, u32[]{:S(2)}) collective-permute-start(f16[64,640]{1,0:T(8,128)(2,1)S(1)} %get-tuple-element.51), channel_id=1, source_target_pairs={{0,128},{64,192},{128,0},{192,64},{1,129},{65,193},{129,1},{193,65... | collective-permute-start | bytes 245768 | tf_op jit(solution)/shard_map/ppermute | solution.py:19
  125.7 3.1 %collective-permute-done.22 = f16[64,640]{1,0:T(8,128)(2,1)S(1)} collective-permute-done((f16[64,640]{1,0:T(8,128)(2,1)S(1)}, f16[64,640]{1,0:T(8,128)(2,1)S(1)}, u32[]{:S(2)}, u32[]{:S(2)}) %collective-permute-start.22) | collective-permute-done | bytes 81952 | tf_op jit(solution)/shard_map/ppermute | solution.py:19
  131.5 17.8 %all_to_all.26 = f16[64,16,128]{2,1,0:T(8,128)(2,1)S(1)} all-to-all(f16[64,16,128]{2,1,0:T(8,128)(2,1)S(1)} %bitcast.170), channel_id=1, replica_groups=mesh['x'=4,'c'=2,'z'=8,'y'=4] {'x','c','z'}, dimensions={0} | all-to-all | bytes 524288 | tf_op jit(solution)/shard_map/all_to_all | solution.py:66
  149.5 14.7 %all_to_all.27 = f16[8,128,128]{2,1,0:T(8,128)(2,1)S(1)} all-to-all(f16[8,128,128]{2,1,0:T(8,128)(2,1)S(1)} %broadcast_in_dim.88), channel_id=1, replica_groups=mesh['x'=4,'c'=2,'z'=8,'y'=4] {'z'}, dimensions={0} | all-to-all | bytes 524288 | tf_op jit(solution)/shard_map/all_to_all | solution.py:66
  170.8 2.6 %collective-permute-start.27 = (f16[512,128]{1,0:T(8,128)(2,1)S(1)}, f16[512,128]{1,0:T(8,128)(2,1)S(1)}, u32[]{:S(2)}, u32[]{:S(2)}) collective-permute-start(f16[512,128]{1,0:T(8,128)(2,1)S(1)} %slice.154), channel_id=1, source_target_pairs={{0,1},{1,2},{2,3},{3,0},{4,5},{5,6},{6,7},{7,4},{8,9},{9,10},{10,1... | collective-permute-start | bytes 393224 | tf_op jit(solution)/shard_map/ppermute | solution.py:19
  175.9 3.8 %collective-permute-done.28 = f16[512,128]{1,0:T(8,128)(2,1)S(1)} collective-permute-done((f16[512,128]{1,0:T(8,128)(2,1)S(1)}, f16[512,128]{1,0:T(8,128)(2,1)S(1)}, u32[]{:S(2)}, u32[]{:S(2)}) %collective-permute-start.28) | collective-permute-done | bytes 131104 | tf_op jit(solution)/shard_map/ppermute | solution.py:19
  181.1 3.0 %shard_map.95 = bf16[128,4096]{1,0:T(8,128)(2,1)} custom-call(f32[4,8,4,2,2,8,128]{6,5,4,3,2,1,0:T(8,128)S(1)} %convert.43.grad_ref, bf16[128,4096]{1,0:T(8,128)(2,1)S(1)} %bitcast.149, f32[1,4096]{1,0:T(1,128)S(1)} %bitcast.151), custom_call_target="tpu_custom_call" | custom-call | flops 4194304 | bytes 4194304 | tf_op jit(solution)/shard_map/pallas_call | solution.py:311
  (120 shorter events, 45.3 us)
Async XLA Ops:
  4.2 20.6 %all-to-all-start = ((bf16[8,528,128]{2,1,0:T(8,128)(2,1)}), bf16[8,528,128]{2,1,0:T(8,128)(2,1)S(1)}, u32[]{:S(2)}, u32[]{:S(2)}) async-start(bf16[8,528,128]{2,1,0:T(8,128)(2,1)} %normed_slices.1), calls=%async_computation | async-start | bytes 2162688 | tf_op jit(solution)/shard_map/all_to_all | solution.py:66
  12.5 35.0 %collective-permute-start = (bf16[501,2048]{1,0:T(8,128)(2,1)}, bf16[501,2048]{1,0:T(8,128)(2,1)}, u32[]{:S(2)}, u32[]{:S(2)}) collective-permute-start(bf16[501,2048]{1,0:T(8,128)(2,1)} %get-tuple-element.36), channel_id=1, source_target_pairs={{0,32},{32,0},{1,33},{33,1},{2,34},{34,2},{3,35},{35,3},{4,36},{36... | collective-permute-start | bytes 6156296 | tf_op jit(solution)/shard_map/ppermute | solution.py:23
  26.6 13.6 %collective-permute-start.5 = (bf16[256,640]{1,0:T(8,128)(2,1)S(1)}, bf16[256,640]{1,0:T(8,128)(2,1)S(1)}, u32[]{:S(2)}, u32[]{:S(2)}) collective-permute-start(bf16[256,640]{1,0:T(8,128)(2,1)S(1)} %get-tuple-element.19), channel_id=1, source_target_pairs={{0,3},{1,0},{2,1},{3,2},{4,7},{5,4},{6,5},{7,6},{8,11},{9,8},{10,9... | collective-permute-start | bytes 983048 | tf_op jit(solution)/shard_map/ppermute | solution.py:19
  27.4 9.0 %collective-permute-start.6 = (bf16[256,640]{1,0:T(8,128)(2,1)S(1)}, bf16[256,640]{1,0:T(8,128)(2,1)S(1)}, u32[]{:S(2)}, u32[]{:S(2)}) collective-permute-start(bf16[256,640]{1,0:T(8,128)(2,1)S(1)} %get-tuple-element.19), channel_id=1, source_target_pairs={{0,1},{1,2},{2,3},{3,0},{4,5},{5,6},{6,7},{7,4},{8,9},{9,10},{10,1... | collective-permute-start | bytes 983048 | tf_op jit(solution)/shard_map/ppermute | solution.py:19
  29.9 11.1 %collective-permute-start.1 = (bf16[256,640]{1,0:T(8,128)(2,1)S(1)}, bf16[256,640]{1,0:T(8,128)(2,1)S(1)}, u32[]{:S(2)}, u32[]{:S(2)}) collective-permute-start(bf16[256,640]{1,0:T(8,128)(2,1)S(1)} %get-tuple-element.18), channel_id=1, source_target_pairs={{0,192},{64,0},{128,64},{192,128},{1,193},{65,1},{129,65},{193,129... | collective-permute-start | bytes 983048 | tf_op jit(solution)/shard_map/ppermute | solution.py:19
  31.1 9.6 %collective-permute-start.2 = (bf16[256,640]{1,0:T(8,128)(2,1)S(1)}, bf16[256,640]{1,0:T(8,128)(2,1)S(1)}, u32[]{:S(2)}, u32[]{:S(2)}) collective-permute-start(bf16[256,640]{1,0:T(8,128)(2,1)S(1)} %get-tuple-element.18), channel_id=1, source_target_pairs={{0,64},{64,128},{128,192},{192,0},{1,65},{65,129},{129,193},{193,1... | collective-permute-start | bytes 983048 | tf_op jit(solution)/shard_map/ppermute | solution.py:19
  36.4 7.8 %collective-permute-start.7 = (bf16[128,640]{1,0:T(8,128)(2,1)S(1)}, bf16[128,640]{1,0:T(8,128)(2,1)S(1)}, u32[]{:S(2)}, u32[]{:S(2)}) collective-permute-start(bf16[128,640]{1,0:T(8,128)(2,1)S(1)} %slice.146), channel_id=1, source_target_pairs={{0,1},{1,2},{2,3},{3,0},{4,5},{5,6},{6,7},{7,4},{8,9},{9,10},{10,1... | collective-permute-start | bytes 491528 | tf_op jit(solution)/shard_map/ppermute | solution.py:19
  40.2 6.6 %collective-permute-start.8 = (bf16[128,640]{1,0:T(8,128)(2,1)S(1)}, bf16[128,640]{1,0:T(8,128)(2,1)S(1)}, u32[]{:S(2)}, u32[]{:S(2)}) collective-permute-start(bf16[128,640]{1,0:T(8,128)(2,1)S(1)} %slice.147), channel_id=1, source_target_pairs={{0,3},{1,0},{2,1},{3,2},{4,7},{5,4},{6,5},{7,6},{8,11},{9,8},{10,9... | collective-permute-start | bytes 491528 | tf_op jit(solution)/shard_map/ppermute | solution.py:19
  40.7 6.6 %collective-permute-start.3 = (bf16[128,640]{1,0:T(8,128)(2,1)S(1)}, bf16[128,640]{1,0:T(8,128)(2,1)S(1)}, u32[]{:S(2)}, u32[]{:S(2)}) collective-permute-start(bf16[128,640]{1,0:T(8,128)(2,1)S(1)} %slice.144), channel_id=1, source_target_pairs={{0,64},{64,128},{128,192},{192,0},{1,65},{65,129},{129,193},{193,1... | collective-permute-start | bytes 491528 | tf_op jit(solution)/shard_map/ppermute | solution.py:19
  57.2 16.5 %all-to-all-start.1 = ((f32[8,8,128]{2,1,0:T(8,128)}), f32[8,8,128]{2,1,0:T(8,128)S(1)}, u32[]{:S(2)}, u32[]{:S(2)}) async-start(f32[8,8,128]{2,1,0:T(8,128)} %broadcast_in_dim.85), calls=%async_computation.1 | async-start | bytes 65536 | tf_op jit(solution)/shard_map/all_to_all | solution.py:66
  98.1 7.5 %collective-permute-start.11 = (f16[128,640]{1,0:T(8,128)(2,1)S(1)}, f16[128,640]{1,0:T(8,128)(2,1)S(1)}, u32[]{:S(2)}, u32[]{:S(2)}) collective-permute-start(f16[128,640]{1,0:T(8,128)(2,1)S(1)} %get-tuple-element.52), channel_id=1, source_target_pairs={{0,64},{64,128},{128,192},{192,0},{1,65},{65,129},{129,193},{193,1... | collective-permute-start | bytes 491528 | tf_op jit(solution)/shard_map/ppermute | solution.py:19
  98.9 6.8 %collective-permute-start.13 = (f16[128,640]{1,0:T(8,128)(2,1)S(1)}, f16[128,640]{1,0:T(8,128)(2,1)S(1)}, u32[]{:S(2)}, u32[]{:S(2)}) collective-permute-start(f16[128,640]{1,0:T(8,128)(2,1)S(1)} %get-tuple-element.53), channel_id=1, source_target_pairs={{0,192},{64,0},{128,64},{192,128},{1,193},{65,1},{129,65},{193,129... | collective-permute-start | bytes 491528 | tf_op jit(solution)/shard_map/ppermute | solution.py:19
  101.6 7.7 %collective-permute-start.18 = (f16[128,640]{1,0:T(8,128)(2,1)S(1)}, f16[128,640]{1,0:T(8,128)(2,1)S(1)}, u32[]{:S(2)}, u32[]{:S(2)}) collective-permute-start(f16[128,640]{1,0:T(8,128)(2,1)S(1)} %get-tuple-element.54), channel_id=1, source_target_pairs={{0,1},{1,2},{2,3},{3,0},{4,5},{5,6},{6,7},{7,4},{8,9},{9,10},{10,1... | collective-permute-start | bytes 491528 | tf_op jit(solution)/shard_map/ppermute | solution.py:19
  103.6 6.6 %collective-permute-start.20 = (f16[128,640]{1,0:T(8,128)(2,1)S(1)}, f16[128,640]{1,0:T(8,128)(2,1)S(1)}, u32[]{:S(2)}, u32[]{:S(2)}) collective-permute-start(f16[128,640]{1,0:T(8,128)(2,1)S(1)} %get-tuple-element.55), channel_id=1, source_target_pairs={{0,3},{1,0},{2,1},{3,2},{4,7},{5,4},{6,5},{7,6},{8,11},{9,8},{10,9... | collective-permute-start | bytes 491528 | tf_op jit(solution)/shard_map/ppermute | solution.py:19
  105.9 10.2 %collective-permute-start.12 = (f16[256,640]{1,0:T(8,128)(2,1)S(1)}, f16[256,640]{1,0:T(8,128)(2,1)S(1)}, u32[]{:S(2)}, u32[]{:S(2)}) collective-permute-start(f16[256,640]{1,0:T(8,128)(2,1)S(1)} %pad_maximum_fusion), channel_id=1, source_target_pairs={{0,64},{64,128},{128,192},{192,0},{1,65},{65,129},{129,193},{193,1... | collective-permute-start | bytes 983048 | tf_op jit(solution)/shard_map/ppermute | solution.py:19
  106.1 10.0 %collective-permute-start.14 = (f16[256,640]{1,0:T(8,128)(2,1)S(1)}, f16[256,640]{1,0:T(8,128)(2,1)S(1)}, u32[]{:S(2)}, u32[]{:S(2)}) collective-permute-start(f16[256,640]{1,0:T(8,128)(2,1)S(1)} %pad_maximum_fusion.1), channel_id=1, source_target_pairs={{0,192},{64,0},{128,64},{192,128},{1,193},{65,1},{129,65},{193,129... | collective-permute-start | bytes 983048 | tf_op jit(solution)/shard_map/ppermute | solution.py:19
  110.4 9.6 %collective-permute-start.19 = (f16[256,640]{1,0:T(8,128)(2,1)S(1)}, f16[256,640]{1,0:T(8,128)(2,1)S(1)}, u32[]{:S(2)}, u32[]{:S(2)}) collective-permute-start(f16[256,640]{1,0:T(8,128)(2,1)S(1)} %pad_maximum_fusion.2), channel_id=1, source_target_pairs={{0,1},{1,2},{2,3},{3,0},{4,5},{5,6},{6,7},{7,4},{8,9},{9,10},{10,1... | collective-permute-start | bytes 983048 | tf_op jit(solution)/shard_map/ppermute | solution.py:19
  111.6 10.4 %collective-permute-start.21 = (f16[256,640]{1,0:T(8,128)(2,1)S(1)}, f16[256,640]{1,0:T(8,128)(2,1)S(1)}, u32[]{:S(2)}, u32[]{:S(2)}) collective-permute-start(f16[256,640]{1,0:T(8,128)(2,1)S(1)} %pad_maximum_fusion.3), channel_id=1, source_target_pairs={{0,3},{1,0},{2,1},{3,2},{4,7},{5,4},{6,5},{7,6},{8,11},{9,8},{10,9... | collective-permute-start | bytes 983048 | tf_op jit(solution)/shard_map/ppermute | solution.py:19
  116.3 8.5 %collective-permute-start.15 = (f16[64,640]{1,0:T(8,128)(2,1)S(1)}, f16[64,640]{1,0:T(8,128)(2,1)S(1)}, u32[]{:S(2)}, u32[]{:S(2)}) collective-permute-start(f16[64,640]{1,0:T(8,128)(2,1)S(1)} %get-tuple-element.46), channel_id=1, source_target_pairs={{0,1},{1,2},{2,3},{3,0},{4,5},{5,6},{6,7},{7,4},{8,9},{9,10},{10,1... | collective-permute-start | bytes 245768 | tf_op jit(solution)/shard_map/ppermute | solution.py:19
  118.4 7.2 %collective-permute-start.16 = (f16[64,640]{1,0:T(8,128)(2,1)S(1)}, f16[64,640]{1,0:T(8,128)(2,1)S(1)}, u32[]{:S(2)}, u32[]{:S(2)}) collective-permute-start(f16[64,640]{1,0:T(8,128)(2,1)S(1)} %get-tuple-element.48), channel_id=1, source_target_pairs={{0,2},{1,3},{2,0},{3,1},{4,6},{5,7},{6,4},{7,5},{8,10},{9,11},{10,... | collective-permute-start | bytes 245768 | tf_op jit(solution)/shard_map/ppermute | solution.py:19
  122.2 6.6 %collective-permute-start.22 = (f16[64,640]{1,0:T(8,128)(2,1)S(1)}, f16[64,640]{1,0:T(8,128)(2,1)S(1)}, u32[]{:S(2)}, u32[]{:S(2)}) collective-permute-start(f16[64,640]{1,0:T(8,128)(2,1)S(1)} %get-tuple-element.49), channel_id=1, source_target_pairs={{0,64},{64,128},{128,192},{192,0},{1,65},{65,129},{129,193},{193,1... | collective-permute-start | bytes 245768 | tf_op jit(solution)/shard_map/ppermute | solution.py:19
  122.3 6.5 %collective-permute-start.23 = (f16[64,640]{1,0:T(8,128)(2,1)S(1)}, f16[64,640]{1,0:T(8,128)(2,1)S(1)}, u32[]{:S(2)}, u32[]{:S(2)}) collective-permute-start(f16[64,640]{1,0:T(8,128)(2,1)S(1)} %get-tuple-element.51), channel_id=1, source_target_pairs={{0,128},{64,192},{128,0},{192,64},{1,129},{65,193},{129,1},{193,65... | collective-permute-start | bytes 245768 | tf_op jit(solution)/shard_map/ppermute | solution.py:19
  164.2 6.6 %collective-permute-start.26 = (f16[1024,128]{1,0:T(8,128)(2,1)S(1)}, f16[1024,128]{1,0:T(8,128)(2,1)S(1)}, u32[]{:S(2)}, u32[]{:S(2)}) collective-permute-start(f16[1024,128]{1,0:T(8,128)(2,1)S(1)} %bitcast.166), channel_id=1, source_target_pairs={{0,1},{1,2},{2,3},{3,0},{4,5},{5,6},{6,7},{7,4},{8,9},{9,10},{10,1... | collective-permute-start | bytes 786440 | tf_op jit(solution)/shard_map/ppermute | solution.py:19
  165.7 7.7 %collective-permute-start.25 = (f16[1024,128]{1,0:T(8,128)(2,1)S(1)}, f16[1024,128]{1,0:T(8,128)(2,1)S(1)}, u32[]{:S(2)}, u32[]{:S(2)}) collective-permute-start(f16[1024,128]{1,0:T(8,128)(2,1)S(1)} %bitcast.167), channel_id=1, source_target_pairs={{0,3},{1,0},{2,1},{3,2},{4,7},{5,4},{6,5},{7,6},{8,11},{9,8},{10,9... | collective-permute-start | bytes 786440 | tf_op jit(solution)/shard_map/ppermute | solution.py:19
  (12 other events, 55.6 us)

commit v2 on v1

--- a/solution.py
+++ b/solution.py
@@ -154,13 +154,17 @@
     spot = iota((8, 128), 0) * 128 + iota((8, 128), 1)
     coef_ref[...] = jnp.where(spot.astype(F32) < count, loss_scale_ref[0] / count, 0.0)
     count_ref[...] = jnp.broadcast_to(count, (8, 128))
-    for n in range(4):
+    acc[...] = jnp.zeros_like(acc)
+
+    def add(n, carry):
         values = jnp.concatenate([packed_ref[2 * n], packed_ref[2 * n + 1]], 1)
         places = [
-            jnp.where(iota((LIVE, 128), 0) == column[m : m + 1], 1.0, 0.0).astype(BF16) for m in (2 * n, 2 * n + 1)
+            jnp.where(iota((LIVE, 128), 0) == column_ref[pl.ds(2 * n + k, 1), :], 1.0, 0.0).astype(BF16) for k in range(2)
         ]
-        part = lax.dot_general(values, jnp.concatenate(places, 1), NT, preferred_element_type=F32)
-        acc[...] = part if n == 0 else acc[...] + part
+        acc[...] += lax.dot_general(values, jnp.concatenate(places, 1), NT, preferred_element_type=F32)
+        return carry
+
+    lax.fori_loop(0, 4, add, 0)
     one_ref[...] = acc[0:256, :].astype(BF16)
     two_ref[...] = acc[256:512, :].astype(BF16)
     word = acc[512:513, :] + 256.0 * acc[513:514, :] + 65536.0 * acc[514:515, :]
@@ -280,9 +284,9 @@
 
 def finish_kernel(grad_ref, h_ref, gain_ref, out_ref, turned):
     slots, width = h_ref.shape
-    for core in range(2):
-        for part in range(2):
-            for a in range(4):
+    def turn(a, carry):
+        for core in range(2):
+            for part in range(2):
                 for b in range(2):
                     blocks = []
                     for pair in range(2):
@@ -291,7 +295,10 @@
                             y, x = (other, a) if part == 0 else (a, other)
                             blocks.append(grad_ref[y, z, x, core, part])
                     at = core * (width // 2) + part * (width // 4) + a * 256 + b * 128
-                    turned[:, at : at + 128] = jnp.concatenate(blocks, 0).T
+                    turned[:, pl.ds(pl.multiple_of(at, 128), 128)] = jnp.concatenate(blocks, 0).T
+        return carry
+
+    lax.fori_loop(0, 4, turn, 0)
 
     def step(i, carry):
         at = pl.ds(pl.multiple_of(i * 16, 16), 16)
@@ -364,8 +371,12 @@
     spread = lax.dot_general(
         chunk, select.astype(F32), NT, precision=lax.Precision.HIGHEST, preferred_element_type=F32
     )
-    spread = spread.astype(F16).reshape(8, 16, 8, slots).transpose(2, 0, 1, 3).reshape(64, 16, slots)
-    spread = exchange(spread, ("x", "c", "z")).reshape(8, 8, 16, slots)
+    spread = spread.astype(F16).reshape(8, 16, 4, 2, slots).transpose(3, 2, 0, 1, 4)
+    kept = lax.dynamic_index_in_dim(spread, core, 0, keepdims=False)
+    came = swap_cores(lax.dynamic_index_in_dim(spread, 1 - core, 0, keepdims=False))
+    low = core == 0
+    spread = jnp.stack([jnp.where(low, kept, came), jnp.where(low, came, kept)], 2)
+    spread = exchange(spread.reshape(32, 32, slots), ("x", "z")).reshape(4, 8, 32, slots)
     spread = jnp.sum(spread.astype(F32), axis=1).astype(F16).reshape(128, slots)
     full = everyone(spread, ("z",)).reshape(1024, slots)
     full = place(gather_ring(full, "y"), "y").astype(F32).reshape(4, 8, 4, 2, 2, 8, slots)

time: 186 us -> 188 us (1.011)
  waiting for transfers between devices: 49 us -> 51.2 us
  blocking collectives: 46.2 us -> 44.2 us
    all_to_all x3, blocking collectives: 46.2 us -> 44.2 us  [exchange(): return lax.all_to_all(value, axes, 0, 0)]
    ppermute x3 -> x4, waiting for transfers between devices: 2.73 us -> 4.06 us  [swap_cores(): return lax.ppermute(value, 'c', [(0, 1), (1, 0)])]
  transfers between devices with their start and end apart: 31 -> 32, of which waited for: 17 -> 19; matrix products, arithmetic and copies ran while one was open for 4% -> 4% of each run, Pallas kernels for 2% -> 2%
where the time goes in v2:
time: 188 us; the launch traced here: 187 us
  waiting for transfers between devices  51.2 us (27%)
  starting transfers between devices  48.6 us (26%)
  blocking collectives  44.2 us (24%)
  Pallas kernels  21.9 us (12%)
  local copies, waits for them, and re-layouts  11.5 us (6%)
  between operations  4.78 us (3%)
  other arithmetic  3.31 us (2%)
    all_to_all x3, blocking collectives, exchange(): return lax.all_to_all(value, axes, 0, 0)  44.2 us
    ppermute x26, starting transfers between devices, shift(): return lax.ppermute(value, axis, [(i, (i + by) % n) for i in range(n)])  34.8 us
    ppermute x26, waiting for transfers between devices, shift(): return lax.ppermute(value, axis, [(i, (i + by) % n) for i in range(n)])  28.1 us
    all_to_all x2, waiting for transfers between devices, exchange(): return lax.all_to_all(value, axes, 0, 0)  19.1 us
    all_to_all x2, starting transfers between devices, exchange(): return lax.all_to_all(value, axes, 0, 0)  12.8 us
    pallas_call x1, Pallas kernels, pull(): pl.pallas_call(pull_kernel, name='pull', out_shape=jax.ShapeDtypeStruct((...  5.68 us
    pallas_call x2, Pallas kernels, product(): pl.pallas_call(product_kernel, name='product', out_shape=jax.ShapeDtypeSt...  5.22 us
    dynamic_slice x1, local copies, waits for them, and re-layouts, body(): lax.dynamic_slice_in_dim(late_weight, (1 - core) * half, half, 1)  4.08 us
  transfers between devices with their start and end apart: 32, of which 19 were waited for; matrix products, arithmetic and copies ran while one was open for 4% of the time, Pallas kernels for 2%

profile of v2, /device:TPU:24, one launch (start us, length us, event | category | flops | bytes accessed | tf_op | source)
XLA Modules:
  0.0 187.2 jit_solution(17608966882884976812)
XLA Ops:
  0.6 3.6 %normed_slices.1 = bf16[8,528,128]{2,1,0:T(8,128)(2,1)} custom-call(s32[1]{0:T(128)} %bitcast.2.y_ref, bf16[128,4096]{1,0:T(8,128)(2,1)} %bitcast.159, f32[1,4096]{1,0:T(1,128)} %bitcast.161, s32[1,128]{1,0:T(1,128)} %target_ref.1, s32[1,128]{1,0:T(1,128)} %mask_ref.1, s32[1,128]{1,0:T(1,128)} %position_ref.1), custom_call_target="tpu_custom_call" | custom-call | flops 2097152 | bytes 2097152 | tf_op jit(solution)/shard_map/normed_slices/pallas_call | solution.py:124
  4.2 4.3 %all-to-all-start = ((bf16[8,528,128]{2,1,0:T(8,128)(2,1)}), bf16[8,528,128]{2,1,0:T(8,128)(2,1)S(1)}, u32[]{:S(2)}, u32[]{:S(2)}) async-start(bf16[8,528,128]{2,1,0:T(8,128)(2,1)} %normed_slices.1), calls=%async_computation | async-start | bytes 2162688 | tf_op jit(solution)/shard_map/all_to_all | solution.py:66
  8.5 4.1 %constant_dynamic-slice_fusion.2 = (bf16[501,2048]{1,0:T(8,128)(2,1)}, bf16[501,2048]{1,0:T(8,128)(2,1)S(1)}) fusion(bf16[501,4096]{1,0:T(8,128)(2,1)} %param.10, s32[]{:T(128)S(6)} %select_n.160, s32[]{:T(128)S(6)} %select_n.159), kind=kLoop, calls=%fused_computation.84 | loop fusion | bytes 8208392 | tf_op jit(solution)/shard_map/dynamic_slice | solution.py:346
  13.8 11.1 %all-to-all-done.packed_ref = bf16[8,528,128]{2,1,0:T(8,128)(2,1)S(1)} async-done(((bf16[8,528,128]{2,1,0:T(8,128)(2,1)}), bf16[8,528,128]{2,1,0:T(8,128)(2,1)S(1)}, u32[]{:S(2)}, u32[]{:S(2)}) %all-to-all-start) | async-done | bytes 1081376 | tf_op jit(solution)/shard_map/all_to_all | solution.py:66
  33.0 4.1 %collective-permute-done.6 = bf16[256,640]{1,0:T(8,128)(2,1)S(1)} collective-permute-done((bf16[256,640]{1,0:T(8,128)(2,1)S(1)}, bf16[256,640]{1,0:T(8,128)(2,1)S(1)}, u32[]{:S(2)}, u32[]{:S(2)}) %collective-permute-start.6) | collective-permute-done | bytes 327712 | tf_op jit(solution)/shard_map/ppermute | solution.py:19
  37.2 3.8 %collective-permute-start.7 = (bf16[128,640]{1,0:T(8,128)(2,1)S(1)}, bf16[128,640]{1,0:T(8,128)(2,1)S(1)}, u32[]{:S(2)}, u32[]{:S(2)}) collective-permute-start(bf16[128,640]{1,0:T(8,128)(2,1)S(1)} %slice.146), channel_id=1, source_target_pairs={{0,1},{1,2},{2,3},{3,0},{4,5},{5,6},{6,7},{7,4},{8,9},{9,10},{10,1... | collective-permute-start | bytes 491528 | tf_op jit(solution)/shard_map/ppermute | solution.py:19
  41.7 3.1 %collective-permute-start.4 = (bf16[128,640]{1,0:T(8,128)(2,1)S(1)}, bf16[128,640]{1,0:T(8,128)(2,1)S(1)}, u32[]{:S(2)}, u32[]{:S(2)}) collective-permute-start(bf16[128,640]{1,0:T(8,128)(2,1)S(1)} %slice.145), channel_id=1, source_target_pairs={{0,192},{64,0},{128,64},{192,128},{1,193},{65,1},{129,65},{193,129... | collective-permute-start | bytes 491528 | tf_op jit(solution)/shard_map/ppermute | solution.py:19
  45.0 2.6 %collective-permute-done.8 = bf16[128,640]{1,0:T(8,128)(2,1)S(1)} collective-permute-done((bf16[128,640]{1,0:T(8,128)(2,1)S(1)}, bf16[128,640]{1,0:T(8,128)(2,1)S(1)}, u32[]{:S(2)}, u32[]{:S(2)}) %collective-permute-start.8) | collective-permute-done | bytes 163872 | tf_op jit(solution)/shard_map/ppermute | solution.py:19
  48.3 3.4 %product.2 = f32[501,640]{1,0:T(8,128)S(1)} custom-call(bf16[501,2048]{1,0:T(8,128)(2,1)} %collective-permute-done.weight_ref.other_ref, bf16[1024,640]{1,0:T(8,128)(2,1)S(1)} %bitcast.155, bf16[1024,640]{1,0:T(8,128)(2,1)S(1)} %bitcast.157), custom_call_target="tpu_custom_call" | custom-call | flops 1313341440 | bytes 6291456 | tf_op jit(solution)/shard_map/product/pallas_call | solution.py:199
  57.9 8.5 %all-to-all-start.1 = ((f32[8,8,128]{2,1,0:T(8,128)}), f32[8,8,128]{2,1,0:T(8,128)S(1)}, u32[]{:S(2)}, u32[]{:S(2)}) async-start(f32[8,8,128]{2,1,0:T(8,128)} %broadcast_in_dim.85), calls=%async_computation.1 | async-start | bytes 65536 | tf_op jit(solution)/shard_map/all_to_all | solution.py:66
  66.4 8.0 %all-to-all-done.1 = f32[8,8,128]{2,1,0:T(8,128)S(1)} async-done(((f32[8,8,128]{2,1,0:T(8,128)}), f32[8,8,128]{2,1,0:T(8,128)S(1)}, u32[]{:S(2)}, u32[]{:S(2)}) %all-to-all-start.1) | async-done | bytes 32800 | tf_op jit(solution)/shard_map/all_to_all | solution.py:66
  74.5 13.6 %all_to_all.25 = f32[32,8,128]{2,1,0:T(8,128)S(1)} all-to-all(f32[32,8,128]{2,1,0:T(8,128)S(1)} %broadcast_in_dim.86), channel_id=1, replica_groups=mesh['x'=4,'c'=2,'z'=8,'y'=4] {'x','c','y'}, dimensions={0} | all-to-all | bytes 262144 | tf_op jit(solution)/shard_map/all_to_all | solution.py:66
  92.8 5.7 %pull.1 = f32[2048,640]{1,0:T(8,128)S(1)} custom-call(bf16[501,2048]{1,0:T(8,128)(2,1)S(1)} %get-tuple-element.37.weight_ref.mine_ref, bf16[501,2048]{1,0:T(8,128)(2,1)} %collective-permute-done.weight_ref.other_ref, bf16[501,640]{1,0:T(8,128)(2,1)S(1)} %logit_grad.1.grad_ref, bf16[501,640]{1,0:T(8,128)(2,1)S(1)} %collective-permute-done.10.other_grad_ref), custom_call_target="tpu_custom_call" | custom-call | flops 2626682880 | bytes 12582912 | tf_op jit(solution)/shard_map/pull/pallas_call | solution.py:223
  99.7 2.6 %collective-permute-start.13 = (f16[128,640]{1,0:T(8,128)(2,1)S(1)}, f16[128,640]{1,0:T(8,128)(2,1)S(1)}, u32[]{:S(2)}, u32[]{:S(2)}) collective-permute-start(f16[128,640]{1,0:T(8,128)(2,1)S(1)} %get-tuple-element.55), channel_id=1, source_target_pairs={{0,192},{64,0},{128,64},{192,128},{1,193},{65,1},{129,65},{193,129... | collective-permute-start | bytes 491528 | tf_op jit(solution)/shard_map/ppermute | solution.py:19
  106.8 3.3 %collective-permute-start.14 = (f16[256,640]{1,0:T(8,128)(2,1)S(1)}, f16[256,640]{1,0:T(8,128)(2,1)S(1)}, u32[]{:S(2)}, u32[]{:S(2)}) collective-permute-start(f16[256,640]{1,0:T(8,128)(2,1)S(1)} %pad_maximum_fusion.1), channel_id=1, source_target_pairs={{0,192},{64,0},{128,64},{192,128},{1,193},{65,1},{129,65},{193,129... | collective-permute-start | bytes 983048 | tf_op jit(solution)/shard_map/ppermute | solution.py:19
  113.4 3.4 %collective-permute-done.12 = f16[256,640]{1,0:T(8,128)(2,1)S(1)} collective-permute-done((f16[256,640]{1,0:T(8,128)(2,1)S(1)}, f16[256,640]{1,0:T(8,128)(2,1)S(1)}, u32[]{:S(2)}, u32[]{:S(2)}) %collective-permute-start.12) | collective-permute-done | bytes 327712 | tf_op jit(solution)/shard_map/ppermute | solution.py:19
  123.0 2.5 %collective-permute-start.23 = (f16[64,640]{1,0:T(8,128)(2,1)S(1)}, f16[64,640]{1,0:T(8,128)(2,1)S(1)}, u32[]{:S(2)}, u32[]{:S(2)}) collective-permute-start(f16[64,640]{1,0:T(8,128)(2,1)S(1)} %get-tuple-element.51), channel_id=1, source_target_pairs={{0,128},{64,192},{128,0},{192,64},{1,129},{65,193},{129,1},{193,65... | collective-permute-start | bytes 245768 | tf_op jit(solution)/shard_map/ppermute | solution.py:19
  126.5 3.1 %collective-permute-done.22 = f16[64,640]{1,0:T(8,128)(2,1)S(1)} collective-permute-done((f16[64,640]{1,0:T(8,128)(2,1)S(1)}, f16[64,640]{1,0:T(8,128)(2,1)S(1)}, u32[]{:S(2)}, u32[]{:S(2)}) %collective-permute-start.22) | collective-permute-done | bytes 81952 | tf_op jit(solution)/shard_map/ppermute | solution.py:19
  134.7 16.7 %all_to_all.26 = f16[32,32,128]{2,1,0:T(8,128)(2,1)S(1)} all-to-all(f16[32,32,128]{2,1,0:T(8,128)(2,1)S(1)} %bitcast.180), channel_id=1, replica_groups=mesh['x'=4,'c'=2,'z'=8,'y'=4] {'x','z'}, dimensions={0} | all-to-all | bytes 524288 | tf_op jit(solution)/shard_map/all_to_all | solution.py:66
  151.6 13.9 %all_to_all.27 = f16[8,128,128]{2,1,0:T(8,128)(2,1)S(1)} all-to-all(f16[8,128,128]{2,1,0:T(8,128)(2,1)S(1)} %broadcast_in_dim.88), channel_id=1, replica_groups=mesh['x'=4,'c'=2,'z'=8,'y'=4] {'z'}, dimensions={0} | all-to-all | bytes 524288 | tf_op jit(solution)/shard_map/all_to_all | solution.py:66
  170.7 2.5 %collective-permute-done.27 = f16[1024,128]{1,0:T(8,128)(2,1)S(1)} collective-permute-done((f16[1024,128]{1,0:T(8,128)(2,1)S(1)}, f16[1024,128]{1,0:T(8,128)(2,1)S(1)}, u32[]{:S(2)}, u32[]{:S(2)}) %collective-permute-start.27) | collective-permute-done | bytes 262176 | tf_op jit(solution)/shard_map/ppermute | solution.py:19
  175.6 2.7 %collective-permute-done.28 = f16[512,128]{1,0:T(8,128)(2,1)S(1)} collective-permute-done((f16[512,128]{1,0:T(8,128)(2,1)S(1)}, f16[512,128]{1,0:T(8,128)(2,1)S(1)}, u32[]{:S(2)}, u32[]{:S(2)}) %collective-permute-start.28) | collective-permute-done | bytes 131104 | tf_op jit(solution)/shard_map/ppermute | solution.py:19
  178.3 3.0 %collective-permute-done.29 = f16[512,128]{1,0:T(8,128)(2,1)S(1)} collective-permute-done((f16[512,128]{1,0:T(8,128)(2,1)S(1)}, f16[512,128]{1,0:T(8,128)(2,1)S(1)}, u32[]{:S(2)}, u32[]{:S(2)}) %collective-permute-start.29) | collective-permute-done | bytes 131104 | tf_op jit(solution)/shard_map/ppermute | solution.py:19
  182.8 3.3 %shard_map.95 = bf16[128,4096]{1,0:T(8,128)(2,1)} custom-call(f32[4,8,4,2,2,8,128]{6,5,4,3,2,1,0:T(8,128)S(1)} %convert.43.grad_ref, bf16[128,4096]{1,0:T(8,128)(2,1)S(1)} %bitcast.160, f32[1,4096]{1,0:T(1,128)S(1)} %bitcast.162), custom_call_target="tpu_custom_call" | custom-call | flops 4194304 | bytes 4194304 | tf_op jit(solution)/shard_map/pallas_call | solution.py:318
  (126 shorter events, 49.5 us)
Async XLA Ops:
  4.2 20.6 %all-to-all-start = ((bf16[8,528,128]{2,1,0:T(8,128)(2,1)}), bf16[8,528,128]{2,1,0:T(8,128)(2,1)S(1)}, u32[]{:S(2)}, u32[]{:S(2)}) async-start(bf16[8,528,128]{2,1,0:T(8,128)(2,1)} %normed_slices.1), calls=%async_computation | async-start | bytes 2162688 | tf_op jit(solution)/shard_map/all_to_all | solution.py:66
  12.6 35.6 %collective-permute-start = (bf16[501,2048]{1,0:T(8,128)(2,1)}, bf16[501,2048]{1,0:T(8,128)(2,1)}, u32[]{:S(2)}, u32[]{:S(2)}) collective-permute-start(bf16[501,2048]{1,0:T(8,128)(2,1)} %get-tuple-element.36), channel_id=1, source_target_pairs={{0,32},{32,0},{1,33},{33,1},{2,34},{34,2},{3,35},{35,3},{4,36},{36... | collective-permute-start | bytes 6156296 | tf_op jit(solution)/shard_map/ppermute | solution.py:23
  27.3 13.6 %collective-permute-start.5 = (bf16[256,640]{1,0:T(8,128)(2,1)S(1)}, bf16[256,640]{1,0:T(8,128)(2,1)S(1)}, u32[]{:S(2)}, u32[]{:S(2)}) collective-permute-start(bf16[256,640]{1,0:T(8,128)(2,1)S(1)} %get-tuple-element.19), channel_id=1, source_target_pairs={{0,3},{1,0},{2,1},{3,2},{4,7},{5,4},{6,5},{7,6},{8,11},{9,8},{10,9... | collective-permute-start | bytes 983048 | tf_op jit(solution)/shard_map/ppermute | solution.py:19
  28.2 9.0 %collective-permute-start.6 = (bf16[256,640]{1,0:T(8,128)(2,1)S(1)}, bf16[256,640]{1,0:T(8,128)(2,1)S(1)}, u32[]{:S(2)}, u32[]{:S(2)}) collective-permute-start(bf16[256,640]{1,0:T(8,128)(2,1)S(1)} %get-tuple-element.19), channel_id=1, source_target_pairs={{0,1},{1,2},{2,3},{3,0},{4,5},{5,6},{6,7},{7,4},{8,9},{9,10},{10,1... | collective-permute-start | bytes 983048 | tf_op jit(solution)/shard_map/ppermute | solution.py:19
  30.7 11.1 %collective-permute-start.1 = (bf16[256,640]{1,0:T(8,128)(2,1)S(1)}, bf16[256,640]{1,0:T(8,128)(2,1)S(1)}, u32[]{:S(2)}, u32[]{:S(2)}) collective-permute-start(bf16[256,640]{1,0:T(8,128)(2,1)S(1)} %get-tuple-element.18), channel_id=1, source_target_pairs={{0,192},{64,0},{128,64},{192,128},{1,193},{65,1},{129,65},{193,129... | collective-permute-start | bytes 983048 | tf_op jit(solution)/shard_map/ppermute | solution.py:19
  31.8 9.6 %collective-permute-start.2 = (bf16[256,640]{1,0:T(8,128)(2,1)S(1)}, bf16[256,640]{1,0:T(8,128)(2,1)S(1)}, u32[]{:S(2)}, u32[]{:S(2)}) collective-permute-start(bf16[256,640]{1,0:T(8,128)(2,1)S(1)} %get-tuple-element.18), channel_id=1, source_target_pairs={{0,64},{64,128},{128,192},{192,0},{1,65},{65,129},{129,193},{193,1... | collective-permute-start | bytes 983048 | tf_op jit(solution)/shard_map/ppermute | solution.py:19
  37.2 7.8 %collective-permute-start.7 = (bf16[128,640]{1,0:T(8,128)(2,1)S(1)}, bf16[128,640]{1,0:T(8,128)(2,1)S(1)}, u32[]{:S(2)}, u32[]{:S(2)}) collective-permute-start(bf16[128,640]{1,0:T(8,128)(2,1)S(1)} %slice.146), channel_id=1, source_target_pairs={{0,1},{1,2},{2,3},{3,0},{4,5},{5,6},{6,7},{7,4},{8,9},{9,10},{10,1... | collective-permute-start | bytes 491528 | tf_op jit(solution)/shard_map/ppermute | solution.py:19
  41.0 6.6 %collective-permute-start.8 = (bf16[128,640]{1,0:T(8,128)(2,1)S(1)}, bf16[128,640]{1,0:T(8,128)(2,1)S(1)}, u32[]{:S(2)}, u32[]{:S(2)}) collective-permute-start(bf16[128,640]{1,0:T(8,128)(2,1)S(1)} %slice.147), channel_id=1, source_target_pairs={{0,3},{1,0},{2,1},{3,2},{4,7},{5,4},{6,5},{7,6},{8,11},{9,8},{10,9... | collective-permute-start | bytes 491528 | tf_op jit(solution)/shard_map/ppermute | solution.py:19
  41.5 6.6 %collective-permute-start.3 = (bf16[128,640]{1,0:T(8,128)(2,1)S(1)}, bf16[128,640]{1,0:T(8,128)(2,1)S(1)}, u32[]{:S(2)}, u32[]{:S(2)}) collective-permute-start(bf16[128,640]{1,0:T(8,128)(2,1)S(1)} %slice.144), channel_id=1, source_target_pairs={{0,64},{64,128},{128,192},{192,0},{1,65},{65,129},{129,193},{193,1... | collective-permute-start | bytes 491528 | tf_op jit(solution)/shard_map/ppermute | solution.py:19
  57.9 16.5 %all-to-all-start.1 = ((f32[8,8,128]{2,1,0:T(8,128)}), f32[8,8,128]{2,1,0:T(8,128)S(1)}, u32[]{:S(2)}, u32[]{:S(2)}) async-start(f32[8,8,128]{2,1,0:T(8,128)} %broadcast_in_dim.85), calls=%async_computation.1 | async-start | bytes 65536 | tf_op jit(solution)/shard_map/all_to_all | solution.py:66
  98.9 7.5 %collective-permute-start.11 = (f16[128,640]{1,0:T(8,128)(2,1)S(1)}, f16[128,640]{1,0:T(8,128)(2,1)S(1)}, u32[]{:S(2)}, u32[]{:S(2)}) collective-permute-start(f16[128,640]{1,0:T(8,128)(2,1)S(1)} %get-tuple-element.54), channel_id=1, source_target_pairs={{0,64},{64,128},{128,192},{192,0},{1,65},{65,129},{129,193},{193,1... | collective-permute-start | bytes 491528 | tf_op jit(solution)/shard_map/ppermute | solution.py:19
  99.7 6.8 %collective-permute-start.13 = (f16[128,640]{1,0:T(8,128)(2,1)S(1)}, f16[128,640]{1,0:T(8,128)(2,1)S(1)}, u32[]{:S(2)}, u32[]{:S(2)}) collective-permute-start(f16[128,640]{1,0:T(8,128)(2,1)S(1)} %get-tuple-element.55), channel_id=1, source_target_pairs={{0,192},{64,0},{128,64},{192,128},{1,193},{65,1},{129,65},{193,129... | collective-permute-start | bytes 491528 | tf_op jit(solution)/shard_map/ppermute | solution.py:19
  102.4 7.7 %collective-permute-start.18 = (f16[128,640]{1,0:T(8,128)(2,1)S(1)}, f16[128,640]{1,0:T(8,128)(2,1)S(1)}, u32[]{:S(2)}, u32[]{:S(2)}) collective-permute-start(f16[128,640]{1,0:T(8,128)(2,1)S(1)} %get-tuple-element.56), channel_id=1, source_target_pairs={{0,1},{1,2},{2,3},{3,0},{4,5},{5,6},{6,7},{7,4},{8,9},{9,10},{10,1... | collective-permute-start | bytes 491528 | tf_op jit(solution)/shard_map/ppermute | solution.py:19
  104.4 6.6 %collective-permute-start.20 = (f16[128,640]{1,0:T(8,128)(2,1)S(1)}, f16[128,640]{1,0:T(8,128)(2,1)S(1)}, u32[]{:S(2)}, u32[]{:S(2)}) collective-permute-start(f16[128,640]{1,0:T(8,128)(2,1)S(1)} %get-tuple-element.57), channel_id=1, source_target_pairs={{0,3},{1,0},{2,1},{3,2},{4,7},{5,4},{6,5},{7,6},{8,11},{9,8},{10,9... | collective-permute-start | bytes 491528 | tf_op jit(solution)/shard_map/ppermute | solution.py:19
  106.7 10.2 %collective-permute-start.12 = (f16[256,640]{1,0:T(8,128)(2,1)S(1)}, f16[256,640]{1,0:T(8,128)(2,1)S(1)}, u32[]{:S(2)}, u32[]{:S(2)}) collective-permute-start(f16[256,640]{1,0:T(8,128)(2,1)S(1)} %pad_maximum_fusion), channel_id=1, source_target_pairs={{0,64},{64,128},{128,192},{192,0},{1,65},{65,129},{129,193},{193,1... | collective-permute-start | bytes 983048 | tf_op jit(solution)/shard_map/ppermute | solution.py:19
  106.8 10.0 %collective-permute-start.14 = (f16[256,640]{1,0:T(8,128)(2,1)S(1)}, f16[256,640]{1,0:T(8,128)(2,1)S(1)}, u32[]{:S(2)}, u32[]{:S(2)}) collective-permute-start(f16[256,640]{1,0:T(8,128)(2,1)S(1)} %pad_maximum_fusion.1), channel_id=1, source_target_pairs={{0,192},{64,0},{128,64},{192,128},{1,193},{65,1},{129,65},{193,129... | collective-permute-start | bytes 983048 | tf_op jit(solution)/shard_map/ppermute | solution.py:19
  111.2 9.6 %collective-permute-start.19 = (f16[256,640]{1,0:T(8,128)(2,1)S(1)}, f16[256,640]{1,0:T(8,128)(2,1)S(1)}, u32[]{:S(2)}, u32[]{:S(2)}) collective-permute-start(f16[256,640]{1,0:T(8,128)(2,1)S(1)} %pad_maximum_fusion.2), channel_id=1, source_target_pairs={{0,1},{1,2},{2,3},{3,0},{4,5},{5,6},{6,7},{7,4},{8,9},{9,10},{10,1... | collective-permute-start | bytes 983048 | tf_op jit(solution)/shard_map/ppermute | solution.py:19
  112.4 10.4 %collective-permute-start.21 = (f16[256,640]{1,0:T(8,128)(2,1)S(1)}, f16[256,640]{1,0:T(8,128)(2,1)S(1)}, u32[]{:S(2)}, u32[]{:S(2)}) collective-permute-start(f16[256,640]{1,0:T(8,128)(2,1)S(1)} %pad_maximum_fusion.3), channel_id=1, source_target_pairs={{0,3},{1,0},{2,1},{3,2},{4,7},{5,4},{6,5},{7,6},{8,11},{9,8},{10,9... | collective-permute-start | bytes 983048 | tf_op jit(solution)/shard_map/ppermute | solution.py:19
  117.1 8.5 %collective-permute-start.15 = (f16[64,640]{1,0:T(8,128)(2,1)S(1)}, f16[64,640]{1,0:T(8,128)(2,1)S(1)}, u32[]{:S(2)}, u32[]{:S(2)}) collective-permute-start(f16[64,640]{1,0:T(8,128)(2,1)S(1)} %get-tuple-element.46), channel_id=1, source_target_pairs={{0,1},{1,2},{2,3},{3,0},{4,5},{5,6},{6,7},{7,4},{8,9},{9,10},{10,1... | collective-permute-start | bytes 245768 | tf_op jit(solution)/shard_map/ppermute | solution.py:19
  119.2 7.2 %collective-permute-start.16 = (f16[64,640]{1,0:T(8,128)(2,1)S(1)}, f16[64,640]{1,0:T(8,128)(2,1)S(1)}, u32[]{:S(2)}, u32[]{:S(2)}) collective-permute-start(f16[64,640]{1,0:T(8,128)(2,1)S(1)} %get-tuple-element.48), channel_id=1, source_target_pairs={{0,2},{1,3},{2,0},{3,1},{4,6},{5,7},{6,4},{7,5},{8,10},{9,11},{10,... | collective-permute-start | bytes 245768 | tf_op jit(solution)/shard_map/ppermute | solution.py:19
  123.0 6.6 %collective-permute-start.22 = (f16[64,640]{1,0:T(8,128)(2,1)S(1)}, f16[64,640]{1,0:T(8,128)(2,1)S(1)}, u32[]{:S(2)}, u32[]{:S(2)}) collective-permute-start(f16[64,640]{1,0:T(8,128)(2,1)S(1)} %get-tuple-element.49), channel_id=1, source_target_pairs={{0,64},{64,128},{128,192},{192,0},{1,65},{65,129},{129,193},{193,1... | collective-permute-start | bytes 245768 | tf_op jit(solution)/shard_map/ppermute | solution.py:19
  123.0 6.5 %collective-permute-start.23 = (f16[64,640]{1,0:T(8,128)(2,1)S(1)}, f16[64,640]{1,0:T(8,128)(2,1)S(1)}, u32[]{:S(2)}, u32[]{:S(2)}) collective-permute-start(f16[64,640]{1,0:T(8,128)(2,1)S(1)} %get-tuple-element.51), channel_id=1, source_target_pairs={{0,128},{64,192},{128,0},{192,64},{1,129},{65,193},{129,1},{193,65... | collective-permute-start | bytes 245768 | tf_op jit(solution)/shard_map/ppermute | solution.py:19
  165.5 7.8 %collective-permute-start.27 = (f16[1024,128]{1,0:T(8,128)(2,1)S(1)}, f16[1024,128]{1,0:T(8,128)(2,1)S(1)}, u32[]{:S(2)}, u32[]{:S(2)}) collective-permute-start(f16[1024,128]{1,0:T(8,128)(2,1)S(1)} %bitcast.177), channel_id=1, source_target_pairs={{0,1},{1,2},{2,3},{3,0},{4,5},{5,6},{6,7},{7,4},{8,9},{9,10},{10,1... | collective-permute-start | bytes 786440 | tf_op jit(solution)/shard_map/ppermute | solution.py:19
  167.0 8.1 %collective-permute-start.26 = (f16[1024,128]{1,0:T(8,128)(2,1)S(1)}, f16[1024,128]{1,0:T(8,128)(2,1)S(1)}, u32[]{:S(2)}, u32[]{:S(2)}) collective-permute-start(f16[1024,128]{1,0:T(8,128)(2,1)S(1)} %bitcast.178), channel_id=1, source_target_pairs={{0,3},{1,0},{2,1},{3,2},{4,7},{5,4},{6,5},{7,6},{8,11},{9,8},{10,9... | collective-permute-start | bytes 786440 | tf_op jit(solution)/shard_map/ppermute | solution.py:19
  (13 other events, 57.0 us)
